TPU v7x, 32 devices: a whole 2x2x4 slice. The times are simulated.
32 devices in a mesh: survey: 2 (over x), sector: 16 (over z, y, core).
Axes of the slice: x: 2, y: 2, z: 4, core: 2. Of those that a mesh axis runs over, the one named last changes fastest.
Arguments:
- raw_pings: bfloat16 [32, 512, 2, 1024], P('survey', 'sector'), parts along dimension 0, may hold values from -6 to 6
- focus_matrix: bfloat16 [2, 2048, 512], replicated, may hold values from -0.25 to 0.25
- start_angle: int32 [32], P('survey'), parts along dimension 0, may hold values from 0 to 2047
- ping_count: int32 [32], P('survey'), parts along dimension 0, may hold values from 256 to 512, as said below
Outputs:
- coherence: float32 [32, 2048, 1024], P(('survey', 'sector')), parts along dimension 0
- interferogram: bfloat16 [32, 2, 2048, 1024], P(('survey', 'sector')), parts along dimension 0
There are 2 independent parts, one for each index of `survey`. A program takes and returns all parts, laid end to end along the dimension named above; an argument that names none is the same for every part. Nothing has to cross between parts.
Inputs may be any that keep to these rules, and one draw needn't show every extreme that they name: `ping_count`: every value lies between 256 and 512, and at least one sector holds all 512 pings.
All inputs are finite; a program needn't handle non-finite values.
Results may differ from a plain program's by a relative error of at most 0.0057.
Values may be sent and summed in bfloat16 or wider, within the bound.
No kernel may reach another device: no remote copies, remote signals or barrier semaphores. Data moves between devices by JAX's collectives and lax.ppermute only.
A program may use at most 192 MiB of HBM per device.

v0:
```python
import jax
import jax.numpy as jnp
from jax import lax
from jax.sharding import PartitionSpec as P

WIN = 9


def shifted(block, axis, distance):
    devices = range(lax.axis_size(axis))
    route = [((i - distance) % len(devices), i) for i in devices]
    return lax.ppermute(block, axis, route)


def focus_sector(raw, angle_step, valid_pings, stacked):
    pings_here = raw.shape[0]
    ranges_here = raw.shape[2]
    columns_count = stacked.shape[0] // 2
    ping_mask = (jnp.arange(pings_here, dtype=jnp.int32) < valid_pings).astype(jnp.bfloat16)
    masked = raw * ping_mask[:, None, None]
    product = jnp.dot(
        stacked, masked.reshape(pings_here, 2 * ranges_here), preferred_element_type=jnp.float32
    )
    product = product.reshape(2, columns_count, 2, ranges_here)
    real_part = product[0, :, 0] - product[1, :, 1]
    imag_part = product[0, :, 1] + product[1, :, 0]
    columns = jnp.arange(columns_count, dtype=jnp.int32)
    turn_index = angle_step * columns % columns_count
    phase_turn = 2.0 * jnp.pi / columns_count * turn_index.astype(jnp.float32)
    cosine = jnp.cos(phase_turn)[:, None]
    sine_part = jnp.sin(phase_turn)[:, None]
    mean_power = jnp.mean(real_part * real_part + imag_part * imag_part, axis=0)
    inverse_rms = lax.rsqrt(mean_power + 1e-06)
    turned_real = (real_part * cosine + imag_part * sine_part) * inverse_rms
    turned_imag = (imag_part * cosine - real_part * sine_part) * inverse_rms
    return jnp.stack([turned_real, turned_imag], axis=1).astype(jnp.bfloat16)


def window_sum(field, axis, span):
    half_span = span // 2
    length_axis = field.shape[axis]
    widths = [(0, 0)] * field.ndim
    widths[axis] = (half_span, half_span)
    padded = jnp.pad(field, widths)
    total = lax.slice_in_dim(padded, 0, length_axis, axis=axis)
    for offset in range(1, span):
        total = total + lax.slice_in_dim(padded, offset, offset + length_axis, axis=axis)
    return total


def compare(own_image, other_image, span):
    f_real = own_image[:, 0].astype(jnp.float32)
    f_imag = own_image[:, 1].astype(jnp.float32)
    g_real = other_image[:, 0].astype(jnp.float32)
    g_imag = other_image[:, 1].astype(jnp.float32)
    fields = jnp.stack(
        [
            f_real * g_real + f_imag * g_imag,
            f_imag * g_real - f_real * g_imag,
            f_real * f_real + f_imag * f_imag,
            g_real * g_real + g_imag * g_imag,
        ],
        axis=0,
    )
    looked = window_sum(window_sum(fields, 1, span), 2, span)
    magnitude = jnp.sqrt(looked[0] * looked[0] + looked[1] * looked[1])
    energy = jnp.sqrt(looked[2] * looked[3] + 1e-06)
    coherence = magnitude / energy
    interferogram = (looked[0:2] / float(span * span)).astype(jnp.bfloat16)
    return (coherence, interferogram)


def body(raw_pings, focus_matrix, start_angle, ping_count):
    stacked = focus_matrix.reshape(2 * focus_matrix.shape[1], focus_matrix.shape[2])
    position = lax.axis_index("sector")

    def prepare(pieces, sector):
        return focus_sector(pieces[0], start_angle[sector], ping_count[sector], stacked)[None]

    own_image = (lambda pieces: prepare(pieces, position))(
        lax.all_to_all(raw_pings, "sector", split_axis=0, concat_axis=1, tiled=True)
    )
    other_image = shifted(own_image, "sector", -1)
    coherence, interferogram = compare(own_image[0], other_image[0], WIN)
    return (coherence[None], interferogram[None])


def solution(mesh):
    return jax.shard_map(
        body,
        mesh=mesh,
        in_specs=(P("survey", "sector", None, None), P(), P("survey"), P("survey")),
        out_specs=(P(("survey", "sector"), None, None), P(("survey", "sector"), None, None, None)),
        check_vma=False,
    )
```

profile of v0, /device:TPU:0, one launch (start us, length us, event | category | flops | bytes accessed | tf_op | source)
XLA Modules:
  0.0 722.9 jit_solution(4973740520128592052)
XLA Ops:
  0.6 7.4 %all-to-all-start = ((bf16[16,32,2,1024]{3,2,1,0:T(2,128)(2,1)}), bf16[16,32,2,1024]{3,2,1,0:T(2,128)(2,1)S(1)}, u32[]{:S(2)}, u32[]{:S(2)}) async-start(bf16[16,32,2,1024]{3,2,1,0:T(2,128)(2,1)} %param.4), calls=%async_computation | async-start | bytes 4194304 | tf_op jit(solution)/shard_map/all_to_all | solution.py:81
  8.1 1.2 dynamic_slice.6
  9.3 1.2 dynamic_slice.7
  11.9 37.1 %all-to-all-done = bf16[16,32,2,1024]{3,2,1,0:T(2,128)(2,1)S(1)} async-done(((bf16[16,32,2,1024]{3,2,1,0:T(2,128)(2,1)}), bf16[16,32,2,1024]{3,2,1,0:T(2,128)(2,1)S(1)}, u32[]{:S(2)}, u32[]{:S(2)}) %all-to-all-start) | async-done | bytes 2097184 | tf_op jit(solution)/shard_map/all_to_all | solution.py:81
  49.0 1.9 broadcast_multiply_fusion
  51.5 17.5 %convolution_bitcast_fusion = f32[4096,2048]{0,1:T(8,128)} fusion(bf16[512,2048]{1,0:T(8,128)(2,1)S(1)} %bitcast.52, bf16[4096,512]{1,0:T(8,128)(2,1)} %bitcast.53), kind=kOutput, calls=%fused_computation.23 | convolution fusion | flops 8589934592 | bytes 39845888 | tf_op jit(solution)/shard_map/dot_general | solution.py:21
  69.0 42.6 %reshape.411 = f32[2,2048,2,1024]{1,0,3,2:T(2,128)} reshape(f32[4096,2048]{0,1:T(8,128)} %convolution_bitcast_fusion) | data formatting | bytes 67108864 | tf_op jit(solution)/shard_map/reshape | solution.py:24
  111.7 39.8 %fusion.42 = (f32[1,2048,1,1024]{1,0,3,2:T(1,128)}, f32[1,2048,1,1024]{1,0,3,2:T(1,128)}, f32[1,2048,1,1024]{1,0,3,2:T(1,128)}, f32[1,2048,1,1024]{1,0,3,2:T(1,128)}) fusion(f32[2,2048,2,1024]{1,0,3,2:T(2,128)} %reshape.411), kind=kLoop, calls=%fused_computation.80 | loop fusion | bytes 67108864 | tf_op jit(solution)/shard_map/slice | solution.py:25
  151.5 20.7 %copy.10 = f32[1,2048,1,1024]{3,1,2,0:T(8,128)} copy(f32[1,2048,1,1024]{1,0,3,2:T(1,128)} %get-tuple-element.10) | data formatting | bytes 16777216
  172.3 20.7 %copy.11 = f32[1,2048,1,1024]{3,1,2,0:T(8,128)} copy(f32[1,2048,1,1024]{1,0,3,2:T(1,128)} %get-tuple-element.8) | data formatting | bytes 16777216
  192.9 20.5 %copy.12 = f32[1,2048,1,1024]{3,1,2,0:T(8,128)} copy(f32[1,2048,1,1024]{1,0,3,2:T(1,128)} %get-tuple-element.9) | data formatting | bytes 16777216
  213.5 20.5 %copy.13 = f32[1,2048,1,1024]{3,1,2,0:T(8,128)} copy(f32[1,2048,1,1024]{1,0,3,2:T(1,128)} %get-tuple-element.11) | data formatting | bytes 16777216
  234.0 19.2 %add_reduce_fusion = (f32[1024]{0:T(1024)S(1)}, f32[1,2048,1,1024]{3,1,2,0:T(8,128)}, f32[1,2048,1,1024]{3,1,2,0:T(8,128)}) fusion(f32[1,2048,1,1024]{3,1,2,0:T(8,128)} %copy.12, f32[1,2048,1,1024]{3,1,2,0:T(8,128)} %copy.13, f32[1,2048,1,1024]{3,1,2,0:T(8,128)} %copy.10, f32[1,2048,1,1024]{3,1,2,0:T(8,128)} %copy.11), kind=kLoop, calls=%fused_computation.64 | loop fusion | flops 12581888 | bytes 50335744 | tf_op jit(solution)/shard_map/reduce_sum | solution.py:32
  253.3 8.6 %multiply_convert_fusion.1 = (bf16[1,2048,1,1024]{3,1,2,0:T(8,128)(2,1)S(1)}, bf16[1,2048,1,1024]{3,1,2,0:T(8,128)(2,1)}) fusion(f32[1,2048,1,1024]{3,1,2,0:T(8,128)} %get-tuple-element.6, f32[1,2048,1,1024]{3,1,2,0:T(8,128)} %get-tuple-element.7, f32[1024]{0:T(1024)S(1)} %add_rsqrt_fusion, f32[2048]{0:T(1024)S(1)} %get-tuple-element.17, ...), kind=kLoop, calls=%fused_computation.63 | loop fusion | flops 20971520 | bytes 25186304 | tf_op jit(solution)/shard_map/convert
  261.9 6.2 pad_maximum_fusion.1
  268.0 9.8 %collective-permute-start = (bf16[1,2048,2,1024]{3,1,2,0:T(8,128)(2,1)}, bf16[1,2048,2,1024]{3,1,2,0:T(8,128)(2,1)S(1)}, u32[]{:S(2)}, u32[]{:S(2)}) collective-permute-start(bf16[1,2048,2,1024]{3,1,2,0:T(8,128)(2,1)} %pad_maximum_fusion.1), channel_id=1, source_target_pairs={{1,0},{2,1},{3,2},{4,3},{5,4},{6,5},{7,6},{8,7},{9,8},{10,9},{11,1... | collective-permute-start | bytes 25165832 | tf_op jit(solution)/shard_map/ppermute | solution.py:12
  277.9 91.3 %collective-permute-done = bf16[1,2048,2,1024]{3,1,2,0:T(8,128)(2,1)S(1)} collective-permute-done((bf16[1,2048,2,1024]{3,1,2,0:T(8,128)(2,1)}, bf16[1,2048,2,1024]{3,1,2,0:T(8,128)(2,1)S(1)}, u32[]{:S(2)}, u32[]{:S(2)}) %collective-permute-start) | collective-permute-done | bytes 8388640 | tf_op jit(solution)/shard_map/ppermute | solution.py:12
  369.2 13.3 %fusion.14 = (f32[1,2048,1024]{2,1,0:T(8,128)}, bf16[2048,1,1024]{2,0,1:T(8,128)(2,1)S(1)}, bf16[2048,1,1024]{2,0,1:T(8,128)(2,1)}) fusion(bf16[2048,2,1024]{2,0,1:T(8,128)(2,1)S(1)} %bitcast.49, f32[1024]{0:T(1024)S(1)} %add_rsqrt_fusion, f32[2048]{0:T(1024)S(1)} %get-tuple-element.17, f32[1,2048,1,1024]{3,1,2,0:T(8,128)} %get-tuple-element.7, ...), kind=kLoop, calls=%fused_computation.37 | loop fusion | flops 35651584 | bytes 41963520 | tf_op jit(solution)/shard_map/add | solution.py:58
  382.5 11.1 %fusion.18 = (f32[1,2048,1024]{2,1,0:T(8,128)}, f32[1,2048,1024]{2,1,0:T(8,128)}, f32[1,2048,1024]{2,1,0:T(8,128)}) fusion(bf16[2048,1,1024]{2,0,1:T(8,128)(2,1)S(1)} %get-tuple-element.3, bf16[2048,1,1024]{2,0,1:T(8,128)(2,1)} %get-tuple-element.4, bf16[2048,2,1024]{2,0,1:T(8,128)(2,1)S(1)} %bitcast.50), kind=kLoop, calls=%fused_computation.41 | loop fusion | flops 27262976 | bytes 41943040 | tf_op jit(solution)/shard_map/sub | solution.py:59
  393.6 23.4 %pad_maximum_fusion = f32[4,2048,1024]{2,1,0:T(8,128)} fusion(f32[1,2048,1024]{2,1,0:T(8,128)} %get-tuple-element.15, f32[1,2048,1024]{2,1,0:T(8,128)} %get-tuple-element.16, f32[1,2048,1024]{2,1,0:T(8,128)} %get-tuple-element.14, f32[1,2048,1024]{2,1,0:T(8,128)} %get-tuple-element.2), kind=kLoop, calls=%fused_computation.16 | loop fusion | flops 25165824 | bytes 67108864 | tf_op jit(solution)/shard_map/stack | solution.py:56
  417.0 131.8 %slice_add_fusion = f32[4,2048,1024]{2,1,0:T(8,128)} fusion(f32[4,2048,1024]{2,1,0:T(8,128)} %pad_maximum_fusion), kind=kLoop, calls=%fused_computation.17 | loop fusion | flops 67108864 | bytes 67108864 | tf_op jit(solution)/shard_map/add | solution.py:47
  548.8 147.7 %fusion.7 = f32[4,2048,1024]{2,1,0:T(8,128)} fusion(f32[4,2048,1024]{2,1,0:T(8,128)} %slice_add_fusion), kind=kLoop, calls=%fused_computation.15 | loop fusion | flops 67108864 | bytes 67108864 | tf_op jit(solution)/shard_map/add | solution.py:47
  696.5 9.6 %fusion.19 = bf16[1,2,2048,1024]{3,2,1,0:T(8,128)(2,1)} fusion(f32[4,2048,1024]{2,1,0:T(8,128)} %fusion.7), kind=kLoop, calls=%fused_computation.42 | loop fusion | flops 8388608 | bytes 25165824 | tf_op jit(solution)/shard_map/broadcast_in_dim | solution.py:85
  706.1 16.7 %fusion.22 = f32[1,2048,1024]{2,1,0:T(8,128)} fusion(f32[4,2048,1024]{2,1,0:T(8,128)} %fusion.7), kind=kLoop, calls=%fused_computation.46 | loop fusion | flops 12582912 | bytes 41943040 | tf_op jit(solution)/shard_map/div | solution.py:68
  (4 shorter events, 2.0 us)
Async XLA Ops:
  0.6 48.4 %all-to-all-start = ((bf16[16,32,2,1024]{3,2,1,0:T(2,128)(2,1)}), bf16[16,32,2,1024]{3,2,1,0:T(2,128)(2,1)S(1)}, u32[]{:S(2)}, u32[]{:S(2)}) async-start(bf16[16,32,2,1024]{3,2,1,0:T(2,128)(2,1)} %param.4), calls=%async_computation | async-start | bytes 4194304 | tf_op jit(solution)/shard_map/all_to_all | solution.py:81
  268.0 101.1 %collective-permute-start = (bf16[1,2048,2,1024]{3,1,2,0:T(8,128)(2,1)}, bf16[1,2048,2,1024]{3,1,2,0:T(8,128)(2,1)S(1)}, u32[]{:S(2)}, u32[]{:S(2)}) collective-permute-start(bf16[1,2048,2,1024]{3,1,2,0:T(8,128)(2,1)} %pad_maximum_fusion.1), channel_id=1, source_target_pairs={{1,0},{2,1},{3,2},{4,3},{5,4},{6,5},{7,6},{8,7},{9,8},{10,9},{11,1... | collective-permute-start | bytes 25165832 | tf_op jit(solution)/shard_map/ppermute | solution.py:12
where the time goes:
time: 726 us; the launch traced here: 723 us
  other arithmetic  391 us (54%)
  local copies, waits for them, and re-layouts  168 us (23%)
  waiting for transfers between devices  128 us (18%)
  matrix products  17.5 us (2%)
  starting transfers between devices  17.3 us (2%)
    add x2, other arithmetic, window_sum(): total + lax.slice_in_dim(padded, offset, offset + length_axis, axis=axis)  280 us
    ppermute x1, waiting for transfers between devices, shifted(): return lax.ppermute(block, axis, route)  91.3 us
    unnamed x5, local copies, waits for them, and re-layouts  83.1 us
    reshape x1, local copies, waits for them, and re-layouts, focus_sector(): product = product.reshape(2, columns_count, 2, ranges_here)  42.6 us
    slice x1, local copies, waits for them, and re-layouts, focus_sector(): real_part = product[0, :, 0] - product[1, :, 1]  39.8 us
    all_to_all x1, waiting for transfers between devices, body(): lax.all_to_all(raw_pings, 'sector', split_axis=0, concat_axis=1, tiled=True)  37.1 us
    another operation x1, other arithmetic, compare(): jnp.stack([f_real * g_real + f_imag * g_imag, f_imag * g_real - f_real *...  23.4 us
    reduce_sum x1, other arithmetic, focus_sector(): mean_power = jnp.mean(real_part * real_part + imag_part * imag_part, axis=0)  19.2 us
  transfers between devices with their start and end apart: 2, of which 2 were waited for; matrix products, arithmetic and copies ran while one was open for 1% of the time, Pallas kernels for 0%

commit v1 on v0

v1 whole, which is shorter than its diff:
```python
import functools

import jax
import jax.numpy as jnp
from jax import lax
from jax.experimental import pallas as pl
from jax.experimental.pallas import tpu as pltpu
from jax.sharding import PartitionSpec as P

WIN = 9
LANES = 128
CHUNK = 256
VMEM_LIMIT = 62 * 2**20


def shifted(block, axis, distance):
    devices = range(lax.axis_size(axis))
    route = [((i - distance) % len(devices), i) for i in devices]
    return lax.ppermute(block, axis, route)


def load_operand(xr_ref, xi_ref, xa_ref, xb_ref):
    real, imag = xr_ref[...], xi_ref[...]
    xa_ref[:, :CHUNK] = real
    xa_ref[:, CHUNK:] = imag
    xb_ref[:, :CHUNK] = -imag
    xb_ref[:, CHUNK:] = real


def focus_rows(h_ref, xa_ref, xb_ref, start, rows):
    own = jnp.dot(h_ref[0, pl.ds(start, rows), :], xa_ref[...], preferred_element_type=jnp.float32)
    return own + jnp.dot(h_ref[1, pl.ds(start, rows), :], xb_ref[...], preferred_element_type=jnp.float32)


def focus_kernel(h_ref, xr_ref, xi_ref, out_ref, xa_ref, xb_ref, *, rows):
    load_operand(xr_ref, xi_ref, xa_ref, xb_ref)

    @pl.loop(0, h_ref.shape[1] // rows)
    def _(block):
        start = pl.multiple_of(block * rows, rows)
        product = focus_rows(h_ref, xa_ref, xb_ref, start, rows)
        out_ref[0, pl.ds(start, rows), :] = product[:, :CHUNK]
        out_ref[1, pl.ds(start, rows), :] = product[:, CHUNK:]


def focus(h, pings, rows=512):
    _, columns, depth = h.shape
    chunks = pings.shape[1] // 2 // CHUNK
    return pl.pallas_call(
        functools.partial(focus_kernel, rows=rows),
        grid=(chunks,),
        in_specs=[
            pl.BlockSpec(h.shape, lambda j: (0, 0, 0), pipeline_mode=pl.Buffered(1)),
            pl.BlockSpec((depth, CHUNK), lambda j: (0, j)),
            pl.BlockSpec((depth, CHUNK), lambda j: (0, chunks + j)),
        ],
        out_specs=pl.BlockSpec((2, columns, CHUNK), lambda j: (0, 0, j)),
        out_shape=jax.ShapeDtypeStruct((2, columns, chunks * CHUNK), jnp.float32),
        scratch_shapes=[pltpu.VMEM((depth, 2 * CHUNK), jnp.bfloat16)] * 2,
        compiler_params=pltpu.CompilerParams(vmem_limit_bytes=VMEM_LIMIT),
        cost_estimate=pl.CostEstimate(
            flops=16 * columns * depth * chunks * CHUNK // 2, bytes_accessed=24 * 2**20, transcendentals=0
        ),
        name="focus",
    )(h, pings, pings)


def band(shape, offset, half):
    row = lax.broadcasted_iota(jnp.int32, shape, 0)
    column = lax.broadcasted_iota(jnp.int32, shape, 1)
    return jnp.where(jnp.abs(row - offset - column) <= half, 1.0, 0.0).astype(jnp.bfloat16)


def compare_kernel(
    h_ref, xr_ref, xi_ref, f_ref, turn_ref, coherence_ref, interferogram_ref,
    xa_ref, xb_ref, field_ref, looked_ref, azimuth_ref, range_ref, scale_ref, *, chunks, rows, span
):
    step = pl.program_id(0)
    columns = h_ref.shape[1]
    area = float(span * span)
    halo = 16

    @pl.when(step == 0)
    def _():
        azimuth_ref[...] = band(azimuth_ref.shape, 0, span // 2)
        range_ref[...] = band(range_ref.shape, LANES, span // 2)
        edge = jnp.zeros(looked_ref.shape[:2] + (LANES,), jnp.bfloat16)
        looked_ref[:, :, :LANES] = edge
        looked_ref[:, :, (LANES + chunks * CHUNK):] = edge

    @pl.when(step < chunks)
    def _():
        load_operand(xr_ref, xi_ref, xa_ref, xb_ref)

        def block_fields(block, sums):
            start = pl.multiple_of(block * rows, rows)
            product = focus_rows(h_ref, xa_ref, xb_ref, start, rows)
            here = pl.ds(start, rows)
            f_real, f_imag = f_ref[0, here, :], f_ref[1, here, :]
            g_real, g_imag = product[:, :CHUNK], product[:, CHUNK:]
            cosine = jnp.concatenate([turn_ref[0, here, :]] * (CHUNK // LANES), axis=1)
            sine = jnp.concatenate([turn_ref[1, here, :]] * (CHUNK // LANES), axis=1)
            real = f_real * g_real + f_imag * g_imag
            imag = f_imag * g_real - f_real * g_imag
            f_power = f_real * f_real + f_imag * f_imag
            g_power = g_real * g_real + g_imag * g_imag
            field_ref[0, here, :] = (real * cosine + imag * sine).astype(jnp.bfloat16)
            field_ref[1, here, :] = (imag * cosine - real * sine).astype(jnp.bfloat16)
            field_ref[2, here, :] = f_power.astype(jnp.bfloat16)
            field_ref[3, here, :] = g_power.astype(jnp.bfloat16)
            f_sum, g_sum = sums
            return (
                f_sum + jnp.sum(f_power.reshape(rows // 8, 8, CHUNK), axis=0),
                g_sum + jnp.sum(g_power.reshape(rows // 8, 8, CHUNK), axis=0),
            )

        zero = jnp.zeros((8, CHUNK), jnp.float32)
        f_sum, g_sum = lax.fori_loop(0, columns // rows, block_fields, (zero, zero))
        f_scale = lax.rsqrt(jnp.sum(f_sum, axis=0, keepdims=True) / columns + 1e-06)
        g_scale = lax.rsqrt(jnp.sum(g_sum, axis=0, keepdims=True) / columns + 1e-06)
        scale_ref[0:1, :] = f_scale * g_scale / area
        scale_ref[1:2, :] = f_scale * f_scale / area
        scale_ref[2:3, :] = g_scale * g_scale / area
        lanes = pl.ds(pl.multiple_of(LANES + step * CHUNK, LANES), CHUNK)
        size = azimuth_ref.shape[0]
        stride = size - 2 * halo
        weights = azimuth_ref[...]

        def smooth(start, skip):
            for field in range(4):
                total = jnp.dot(weights, field_ref[field, pl.ds(start, size), :], preferred_element_type=jnp.float32)
                scaled = total * scale_ref[max(field - 1, 0):max(field - 1, 0) + 1, :]
                looked_ref[field, pl.ds(start + skip, size - skip), lanes] = scaled.astype(jnp.bfloat16)[skip:]

        smooth(0, 0)

        @pl.loop(1, (columns - size) // stride + 1)
        def _(block):
            smooth(pl.multiple_of(block * stride, halo), halo)

    @pl.when(step > 0)
    def _():
        lanes = pl.ds(pl.multiple_of((step - 1) * CHUNK, LANES), CHUNK + 2 * LANES)

        @pl.loop(0, columns // rows)
        def _(block):
            here = pl.ds(pl.multiple_of(block * rows, rows), rows)
            real, imag, f_power, g_power = (
                jnp.dot(looked_ref[field, here, lanes], range_ref[...], preferred_element_type=jnp.float32)
                for field in range(4)
            )
            interferogram_ref[0, here, :] = real.astype(jnp.bfloat16)
            interferogram_ref[1, here, :] = imag.astype(jnp.bfloat16)
            power = real * real + imag * imag
            energy = f_power * g_power + 1e-06 / (area * area)
            coherence_ref[here, :] = power * lax.rsqrt(jnp.maximum(power * energy, 1e-37))


def compare(h, pings, own, turn, rows=256):
    _, columns, depth = h.shape
    ranges = pings.shape[1] // 2
    chunks = ranges // CHUNK
    last = chunks - 1
    return pl.pallas_call(
        functools.partial(compare_kernel, chunks=chunks, rows=rows, span=WIN),
        grid=(chunks + 1,),
        in_specs=[
            pl.BlockSpec(h.shape, lambda j: (0, 0, 0), pipeline_mode=pl.Buffered(1)),
            pl.BlockSpec((depth, CHUNK), lambda j: (0, jnp.minimum(j, last))),
            pl.BlockSpec((depth, CHUNK), lambda j: (0, chunks + jnp.minimum(j, last))),
            pl.BlockSpec((2, columns, CHUNK), lambda j: (0, 0, jnp.minimum(j, last))),
            pl.BlockSpec(turn.shape, lambda j: (0, 0, 0), pipeline_mode=pl.Buffered(1)),
        ],
        out_specs=[
            pl.BlockSpec((columns, CHUNK), lambda j: (0, jnp.maximum(j - 1, 0))),
            pl.BlockSpec((2, columns, CHUNK), lambda j: (0, 0, jnp.maximum(j - 1, 0))),
        ],
        out_shape=[
            jax.ShapeDtypeStruct((columns, ranges), jnp.float32),
            jax.ShapeDtypeStruct((2, columns, ranges), jnp.bfloat16),
        ],
        scratch_shapes=[
            pltpu.VMEM((depth, 2 * CHUNK), jnp.bfloat16),
            pltpu.VMEM((depth, 2 * CHUNK), jnp.bfloat16),
            pltpu.VMEM((4, columns, CHUNK), jnp.bfloat16),
            pltpu.VMEM((4, columns, ranges + 2 * LANES), jnp.bfloat16),
            pltpu.VMEM((256, 256), jnp.bfloat16),
            pltpu.VMEM((CHUNK + 2 * LANES, CHUNK), jnp.bfloat16),
            pltpu.VMEM((8, CHUNK), jnp.float32),
        ],
        compiler_params=pltpu.CompilerParams(vmem_limit_bytes=VMEM_LIMIT),
        name="compare",
    )(h, pings, pings, own, turn)


def body(raw_pings, focus_matrix, start_angle, ping_count):
    columns = focus_matrix.shape[1]
    sectors = raw_pings.shape[0]
    position = lax.axis_index("sector")
    received = lax.all_to_all(raw_pings, "sector", split_axis=0, concat_axis=1, tiled=True)[0]
    pings = received.shape[0]
    mask = (jnp.arange(pings, dtype=jnp.int32) < ping_count[position]).astype(jnp.bfloat16)
    own_pings = (received * mask[:, None, None]).reshape(pings, -1)
    other_pings = shifted(own_pings, "sector", -1)
    angle = start_angle[position] - start_angle[(position + 1) % sectors]
    index = (angle * jnp.arange(columns, dtype=jnp.int32)) % columns
    phase = 2.0 * jnp.pi / columns * index.astype(jnp.float32)
    turn = jnp.broadcast_to(jnp.stack([jnp.cos(phase), jnp.sin(phase)])[:, :, None], (2, columns, LANES))
    own = focus(focus_matrix, own_pings)
    coherence, interferogram = compare(focus_matrix, other_pings, own, turn)
    return (coherence[None], interferogram[None])


def solution(mesh):
    return jax.shard_map(
        body,
        mesh=mesh,
        in_specs=(P("survey", "sector", None, None), P(), P("survey"), P("survey")),
        out_specs=(P(("survey", "sector"), None, None), P(("survey", "sector"), None, None, None)),
        check_vma=False,
    )
```

time: 726 us -> 138 us (0.19)
  other arithmetic: 391 us -> 2.47 us
  local copies, waits for them, and re-layouts: 168 us -> 3.68 us
  waiting for transfers between devices: 128 us -> 45.3 us
  Pallas kernels: 0 us -> 66.8 us
  matrix products: 17.5 us -> 0 us
    add x3 -> x0, other arithmetic: 293 us -> none  [the longest x2 280 us: window_sum(): total + lax.slice_in_dim(padded, offset, offset + length_axis, axis=axis)]
    ppermute x1, waiting for transfers between devices: 91.3 us -> 5.56 us  [shifted(): return lax.ppermute(block, axis, route)]
    unnamed x5, local copies, waits for them, and re-layouts: 83.1 us -> 0.6 us
    pallas_call x0 -> x2, Pallas kernels: none -> 66.8 us  [the longest x1 50.6 us: compare(): pl.pallas_call(functools.partial(compare_kernel, chunks=chunks, rows=rows...]
    reshape x1 -> x0, local copies, waits for them, and re-layouts: 42.6 us -> none  [focus_sector(): product = product.reshape(2, columns_count, 2, ranges_here)]
    slice x1 -> x0, local copies, waits for them, and re-layouts: 39.8 us -> none  [focus_sector(): real_part = product[0, :, 0] - product[1, :, 1]]
    another operation x3 -> x1, other arithmetic: 38.2 us -> 0.02 us  [body(): jnp.stack([jnp.cos(phase), jnp.sin(phase)])[:, :, None]]
    reduce_sum x1 -> x0, other arithmetic: 19.2 us -> none  [focus_sector(): mean_power = jnp.mean(real_part * real_part + imag_part * imag_part, axis=0)]
  transfers between devices with their start and end apart: 2 -> 2, of which waited for: 2 -> 2; matrix products, arithmetic and copies ran while one was open for 1% -> 2% of each run, Pallas kernels for 0% -> 12%
where the time goes in v1:
time: 138 us; the launch traced here: 137 us
  Pallas kernels  66.8 us (48%)
  waiting for transfers between devices  45.3 us (33%)
  starting transfers between devices  17.3 us (13%)
  local copies, waits for them, and re-layouts  3.68 us (3%)
  other arithmetic  2.47 us (2%)
  between operations  1.91 us (1%)
    pallas_call x1, Pallas kernels, compare(): pl.pallas_call(functools.partial(compare_kernel, chunks=chunks, rows=rows...  50.6 us
    all_to_all x1, waiting for transfers between devices, body(): lax.all_to_all(raw_pings, 'sector', split_axis=0, concat_axis=1, tiled=True)  39.7 us
    pallas_call x1, Pallas kernels, focus(): pl.pallas_call(functools.partial(focus_kernel, rows=rows), grid=(chunks,)...  16.2 us
    ppermute x1, starting transfers between devices, shifted(): return lax.ppermute(block, axis, route)  9.83 us
    all_to_all x1, starting transfers between devices, body(): lax.all_to_all(raw_pings, 'sector', split_axis=0, concat_axis=1, tiled=True)  7.43 us
    ppermute x1, waiting for transfers between devices, shifted(): return lax.ppermute(block, axis, route)  5.56 us
  transfers between devices with their start and end apart: 2, of which 2 were waited for; matrix products, arithmetic and copies ran while one was open for 2% of the time, Pallas kernels for 12%

profile of v1, /device:TPU:0, one launch (start us, length us, event | category | flops | bytes accessed | tf_op | source)
XLA Modules:
  0.0 137.4 jit_solution(16913677147672060424)
XLA Ops:
  0.6 0.0 copy-start.1
  0.6 7.4 %all-to-all-start = ((bf16[16,32,2,1024]{3,2,1,0:T(2,128)(2,1)}), bf16[16,32,2,1024]{3,2,1,0:T(2,128)(2,1)S(1)}, u32[]{:S(2)}, u32[]{:S(2)}) async-start(bf16[16,32,2,1024]{3,2,1,0:T(2,128)(2,1)} %param.4), calls=%async_computation | async-start | bytes 4194304 | tf_op jit(solution)/shard_map/all_to_all | solution.py:200
  8.1 0.0 copy-done.1
  8.1 0.6 dynamic_slice.9
  8.7 0.6 fusion.5
  9.3 39.7 %all-to-all-done = bf16[16,32,2,1024]{3,2,1,0:T(2,128)(2,1)S(1)} async-done(((bf16[16,32,2,1024]{3,2,1,0:T(2,128)(2,1)}), bf16[16,32,2,1024]{3,2,1,0:T(2,128)(2,1)S(1)}, u32[]{:S(2)}, u32[]{:S(2)}) %all-to-all-start) | async-done | bytes 2097184 | tf_op jit(solution)/shard_map/all_to_all | solution.py:200
  49.0 0.6 copy.6
  49.6 0.0 copy-start
  49.7 1.5 %broadcast_multiply_fusion.xr_ref.xi_ref = bf16[512,2048]{1,0:T(8,128)(2,1)} fusion(bf16[512,2048]{1,0:T(8,128)(2,1)S(1)} %bitcast.7, bf16[512]{0:T(512)(128)(2,1)S(1)} %fusion.5), kind=kLoop, calls=%fused_computation | loop fusion | flops 1048576 | bytes 4195328 | tf_op jit(solution)/shard_map/mul | solution.py:203
  51.2 9.8 %collective-permute-start = (bf16[512,2048]{1,0:T(8,128)(2,1)}, bf16[512,2048]{1,0:T(8,128)(2,1)}, u32[]{:S(2)}, u32[]{:S(2)}) collective-permute-start(bf16[512,2048]{1,0:T(8,128)(2,1)} %broadcast_multiply_fusion.xr_ref.xi_ref), channel_id=1, source_target_pairs={{1,0},{2,1},{3,2},{4,3},{5,4},{6,5},{7,6},{8,7},{9,8},{10,9},{11,1... | collective-permute-start | bytes 6291464 | tf_op jit(solution)/shard_map/ppermute | solution.py:19
  61.0 0.0 copy-done
  61.0 0.6 fusion.6
  62.8 0.3 fusion.3
  63.1 16.2 %focus.1.f_ref = f32[2,2048,1024]{2,1,0:T(8,128)} custom-call(bf16[2,2048,512]{2,1,0:T(8,128)(2,1)} %h_ref.3, bf16[512,2048]{1,0:T(8,128)(2,1)} %broadcast_multiply_fusion.xr_ref.xi_ref, bf16[512,2048]{1,0:T(8,128)(2,1)} %broadcast_multiply_fusion.xr_ref.xi_ref), custom_call_target="tpu_custom_call" | custom-call | flops 8589934592 | bytes 25165824 | tf_op jit(solution)/shard_map/focus/pallas_call | solution.py:49
  79.3 5.6 %collective-permute-done.xr_ref.xi_ref = bf16[512,2048]{1,0:T(8,128)(2,1)} collective-permute-done((bf16[512,2048]{1,0:T(8,128)(2,1)}, bf16[512,2048]{1,0:T(8,128)(2,1)}, u32[]{:S(2)}, u32[]{:S(2)}) %collective-permute-start) | collective-permute-done | bytes 2097184 | tf_op jit(solution)/shard_map/ppermute | solution.py:19
  84.9 1.9 %broadcast_in_dim.6.turn_ref = f32[2,2048,128]{2,1,0:T(8,128)} broadcast(f32[2,2048]{1,0:T(2,128)S(1)} %pad_maximum_fusion), dimensions={0,1} | broadcast | bytes 2113536 | tf_op jit(solution)/shard_map/broadcast_in_dim | solution.py:208
  86.8 50.6 %compare.12 = (f32[2048,1024]{1,0:T(8,128)}, bf16[2,2048,1024]{2,1,0:T(8,128)(2,1)}) custom-call(bf16[2,2048,512]{2,1,0:T(8,128)(2,1)} %h_ref.3, bf16[512,2048]{1,0:T(8,128)(2,1)} %collective-permute-done.xr_ref.xi_ref, bf16[512,2048]{1,0:T(8,128)(2,1)} %collective-permute-done.xr_ref.xi_ref, f32[2,2048,1024]{2,1,0:T(8,128)} %focus.1.f_ref, ...), custom_call_target="tpu_custom_call" | custom-call | tf_op jit(solution)/shard_map/compare/pallas_call | solution.py:164
  (1 shorter events, 0.0 us)
Async XLA Ops:
  0.6 7.5 %copy-start.1 = (s32[16]{0:T(128)S(1)}, s32[16]{0:T(128)}, u32[]{:S(2)}) copy-start(s32[16]{0:T(128)} %param.7) | copy-start | bytes 196
  0.6 48.4 %all-to-all-start = ((bf16[16,32,2,1024]{3,2,1,0:T(2,128)(2,1)}), bf16[16,32,2,1024]{3,2,1,0:T(2,128)(2,1)S(1)}, u32[]{:S(2)}, u32[]{:S(2)}) async-start(bf16[16,32,2,1024]{3,2,1,0:T(2,128)(2,1)} %param.4), calls=%async_computation | async-start | bytes 4194304 | tf_op jit(solution)/shard_map/all_to_all | solution.py:200
  49.6 11.4 %copy-start = (s32[16]{0:T(128)S(1)}, s32[16]{0:T(128)}, u32[]{:S(2)}) copy-start(s32[16]{0:T(128)} %param.6) | copy-start | bytes 196
  51.2 33.7 %collective-permute-start = (bf16[512,2048]{1,0:T(8,128)(2,1)}, bf16[512,2048]{1,0:T(8,128)(2,1)}, u32[]{:S(2)}, u32[]{:S(2)}) collective-permute-start(bf16[512,2048]{1,0:T(8,128)(2,1)} %broadcast_multiply_fusion.xr_ref.xi_ref), channel_id=1, source_target_pairs={{1,0},{2,1},{3,2},{4,3},{5,4},{6,5},{7,6},{8,7},{9,8},{10,9},{11,1... | collective-permute-start | bytes 6291464 | tf_op jit(solution)/shard_map/ppermute | solution.py:19

commit v2 on v1

v2 whole, which is shorter than its diff:
```python
import functools

import jax
import jax.numpy as jnp
from jax import lax
from jax.experimental import pallas as pl
from jax.experimental.pallas import tpu as pltpu
from jax.sharding import PartitionSpec as P

WIN = 9
LANES = 128
CHUNK = 256
VMEM_LIMIT = 62 * 2**20


def shifted(block, axis, distance):
    devices = range(lax.axis_size(axis))
    route = [((i - distance) % len(devices), i) for i in devices]
    return lax.ppermute(block, axis, route)


def load_operand(xr_ref, xi_ref, xa_ref, xb_ref):
    real, imag = xr_ref[...], xi_ref[...]
    xa_ref[:, :CHUNK] = real
    xa_ref[:, CHUNK:] = imag
    xb_ref[:, :CHUNK] = -imag
    xb_ref[:, CHUNK:] = real


def focus_rows(h_ref, xa_ref, xb_ref, start, rows):
    own = jnp.dot(h_ref[0, pl.ds(start, rows), :], xa_ref[...], preferred_element_type=jnp.float32)
    return own + jnp.dot(h_ref[1, pl.ds(start, rows), :], xb_ref[...], preferred_element_type=jnp.float32)


def band(shape, offset, half):
    row = lax.broadcasted_iota(jnp.int32, shape, 0)
    column = lax.broadcasted_iota(jnp.int32, shape, 1)
    return jnp.where(jnp.abs(row - offset - column) <= half, 1.0, 0.0).astype(jnp.bfloat16)


def prepare_windows(azimuth_ref, range_ref, looked_ref):
    azimuth_ref[...] = band(azimuth_ref.shape, 0, WIN // 2)
    range_ref[...] = band(range_ref.shape, LANES, WIN // 2)
    edge = jnp.zeros(looked_ref.shape[:2] + (LANES,), jnp.bfloat16)
    looked_ref[:, :, :LANES] = edge
    looked_ref[:, :, (looked_ref.shape[2] - LANES):] = edge


def azimuth_windows(azimuth_ref, field_ref, looked_ref, step, scales):
    halo = 16
    size = azimuth_ref.shape[0]
    stride = size - 2 * halo
    columns = field_ref.shape[0]
    lanes = pl.ds(pl.multiple_of(LANES + step * CHUNK, LANES), CHUNK)

    def smooth(start, skip):
        total = jnp.dot(azimuth_ref[...], field_ref[pl.ds(start, size), :], preferred_element_type=jnp.float32)
        for field, scale in enumerate(scales):
            scaled = total[:, field * CHUNK:(field + 1) * CHUNK] * scale
            looked_ref[field, pl.ds(start + skip, size - skip), lanes] = scaled.astype(jnp.bfloat16)[skip:]

    smooth(0, 0)

    @pl.loop(1, (columns - size) // stride + 1, unroll=True)
    def _(block):
        smooth(pl.multiple_of(block * stride, halo), halo)


def power_sum(power):
    return jnp.sum(power.reshape(power.shape[0] // 8, 8, power.shape[1]), axis=0)


def inverse_rms(sums, columns):
    return lax.rsqrt(jnp.sum(sums, axis=0, keepdims=True) / columns + 1e-06)


def focus_kernel(
    h_ref, xr_ref, xi_ref, out_ref, inverse_ref, power_ref,
    xa_ref, xb_ref, field_ref, looked_ref, azimuth_ref, range_ref, *, chunks, rows
):
    step = pl.program_id(0)
    columns = h_ref.shape[1]

    @pl.when(step == 0)
    def _():
        prepare_windows(azimuth_ref, range_ref, looked_ref)

    @pl.when(step < chunks)
    def _():
        load_operand(xr_ref, xi_ref, xa_ref, xb_ref)

        def block_fields(block, sums):
            start = pl.multiple_of(block * rows, rows)
            here = pl.ds(start, rows)
            product = focus_rows(h_ref, xa_ref, xb_ref, start, rows)
            real, imag = product[:, :CHUNK], product[:, CHUNK:]
            out_ref[0, here, :] = real
            out_ref[1, here, :] = imag
            power = real * real + imag * imag
            field_ref[here, :] = power.astype(jnp.bfloat16)
            return sums + power_sum(power)

        sums = lax.fori_loop(0, columns // rows, block_fields, jnp.zeros((8, CHUNK), jnp.float32))
        inverse = inverse_rms(sums, columns)
        inverse_ref[...] = jnp.broadcast_to(inverse, inverse_ref.shape)
        azimuth_windows(azimuth_ref, field_ref, looked_ref, step, [inverse * inverse / (WIN * WIN)])

    @pl.when(step > 0)
    def _():
        lanes = pl.ds(pl.multiple_of((step - 1) * CHUNK, LANES), CHUNK + 2 * LANES)

        @pl.loop(0, columns // rows)
        def _(block):
            here = pl.ds(pl.multiple_of(block * rows, rows), rows)
            power_ref[here, :] = jnp.dot(
                looked_ref[0, here, lanes], range_ref[...], preferred_element_type=jnp.float32
            )


def focus(h, pings, rows=2048):
    _, columns, depth = h.shape
    ranges = pings.shape[1] // 2
    chunks = ranges // CHUNK
    last = chunks - 1
    return pl.pallas_call(
        functools.partial(focus_kernel, chunks=chunks, rows=rows),
        grid=(chunks + 1,),
        in_specs=[
            pl.BlockSpec(h.shape, lambda j: (0, 0, 0), pipeline_mode=pl.Buffered(1)),
            pl.BlockSpec((depth, CHUNK), lambda j: (0, jnp.minimum(j, last))),
            pl.BlockSpec((depth, CHUNK), lambda j: (0, chunks + jnp.minimum(j, last))),
        ],
        out_specs=[
            pl.BlockSpec((2, columns, CHUNK), lambda j: (0, 0, jnp.minimum(j, last))),
            pl.BlockSpec((8, CHUNK), lambda j: (0, jnp.minimum(j, last))),
            pl.BlockSpec((columns, CHUNK), lambda j: (0, jnp.maximum(j - 1, 0))),
        ],
        out_shape=[
            jax.ShapeDtypeStruct((2, columns, ranges), jnp.float32),
            jax.ShapeDtypeStruct((8, ranges), jnp.float32),
            jax.ShapeDtypeStruct((columns, ranges), jnp.float32),
        ],
        scratch_shapes=[
            pltpu.VMEM((depth, 2 * CHUNK), jnp.bfloat16),
            pltpu.VMEM((depth, 2 * CHUNK), jnp.bfloat16),
            pltpu.VMEM((columns, CHUNK), jnp.bfloat16),
            pltpu.VMEM((1, columns, ranges + 2 * LANES), jnp.bfloat16),
            pltpu.VMEM((256, 256), jnp.bfloat16),
            pltpu.VMEM((CHUNK + 2 * LANES, CHUNK), jnp.bfloat16),
        ],
        compiler_params=pltpu.CompilerParams(vmem_limit_bytes=VMEM_LIMIT),
        cost_estimate=pl.CostEstimate(
            flops=8 * columns * depth * ranges, bytes_accessed=32 * 2**20, transcendentals=0
        ),
        name="focus",
    )(h, pings, pings)


def compare_kernel(
    h_ref, xr_ref, xi_ref, f_ref, inverse_ref, power_ref, coherence_ref, interferogram_ref,
    xa_ref, xb_ref, field_ref, looked_ref, azimuth_ref, range_ref, *, chunks, rows
):
    step = pl.program_id(0)
    columns = h_ref.shape[1]
    area = float(WIN * WIN)

    @pl.when(step == 0)
    def _():
        prepare_windows(azimuth_ref, range_ref, looked_ref)

    @pl.when(step < chunks)
    def _():
        load_operand(xr_ref, xi_ref, xa_ref, xb_ref)

        def block_fields(block, sums):
            start = pl.multiple_of(block * rows, rows)
            product = focus_rows(h_ref, xa_ref, xb_ref, start, rows)
            here = pl.ds(start, rows)
            f_real, f_imag = f_ref[0, here, :], f_ref[1, here, :]
            g_real, g_imag = product[:, :CHUNK], product[:, CHUNK:]
            power = g_real * g_real + g_imag * g_imag
            field_ref[here, :CHUNK] = (f_real * g_real + f_imag * g_imag).astype(jnp.bfloat16)
            field_ref[here, CHUNK:2 * CHUNK] = (f_imag * g_real - f_real * g_imag).astype(jnp.bfloat16)
            field_ref[here, 2 * CHUNK:] = power.astype(jnp.bfloat16)
            return sums + power_sum(power)

        sums = lax.fori_loop(0, columns // rows, block_fields, jnp.zeros((8, CHUNK), jnp.float32))
        f_scale = inverse_ref[:1, :]
        g_scale = inverse_rms(sums, columns)
        cross = f_scale * g_scale / area
        azimuth_windows(azimuth_ref, field_ref, looked_ref, step, [cross, cross, g_scale * g_scale / area])

    @pl.when(step > 0)
    def _():
        lanes = pl.ds(pl.multiple_of((step - 1) * CHUNK, LANES), CHUNK + 2 * LANES)

        @pl.loop(0, columns // rows)
        def _(block):
            here = pl.ds(pl.multiple_of(block * rows, rows), rows)
            real, imag, g_power = (
                jnp.dot(looked_ref[field, here, lanes], range_ref[...], preferred_element_type=jnp.float32)
                for field in range(3)
            )
            interferogram_ref[0, here, :] = real.astype(jnp.bfloat16)
            interferogram_ref[1, here, :] = imag.astype(jnp.bfloat16)
            power = real * real + imag * imag
            energy = power_ref[here, :] * g_power + 1e-06 / (area * area)
            coherence_ref[here, :] = power * lax.rsqrt(jnp.maximum(power * energy, 1e-37))


def compare(h, pings, own, inverse, power, rows=1024):
    _, columns, depth = h.shape
    ranges = pings.shape[1] // 2
    chunks = ranges // CHUNK
    last = chunks - 1
    return pl.pallas_call(
        functools.partial(compare_kernel, chunks=chunks, rows=rows),
        grid=(chunks + 1,),
        in_specs=[
            pl.BlockSpec(h.shape, lambda j: (0, 0, 0), pipeline_mode=pl.Buffered(1)),
            pl.BlockSpec((depth, CHUNK), lambda j: (0, jnp.minimum(j, last))),
            pl.BlockSpec((depth, CHUNK), lambda j: (0, chunks + jnp.minimum(j, last))),
            pl.BlockSpec((2, columns, CHUNK), lambda j: (0, 0, jnp.minimum(j, last))),
            pl.BlockSpec((8, CHUNK), lambda j: (0, jnp.minimum(j, last))),
            pl.BlockSpec((columns, CHUNK), lambda j: (0, jnp.maximum(j - 1, 0))),
        ],
        out_specs=[
            pl.BlockSpec((columns, CHUNK), lambda j: (0, jnp.maximum(j - 1, 0))),
            pl.BlockSpec((2, columns, CHUNK), lambda j: (0, 0, jnp.maximum(j - 1, 0))),
        ],
        out_shape=[
            jax.ShapeDtypeStruct((columns, ranges), jnp.float32),
            jax.ShapeDtypeStruct((2, columns, ranges), jnp.bfloat16),
        ],
        scratch_shapes=[
            pltpu.VMEM((depth, 2 * CHUNK), jnp.bfloat16),
            pltpu.VMEM((depth, 2 * CHUNK), jnp.bfloat16),
            pltpu.VMEM((columns, 3 * CHUNK), jnp.bfloat16),
            pltpu.VMEM((3, columns, ranges + 2 * LANES), jnp.bfloat16),
            pltpu.VMEM((256, 256), jnp.bfloat16),
            pltpu.VMEM((CHUNK + 2 * LANES, CHUNK), jnp.bfloat16),
        ],
        compiler_params=pltpu.CompilerParams(vmem_limit_bytes=VMEM_LIMIT),
        name="compare",
    )(h, pings, pings, own, inverse, power)


def body(raw_pings, focus_matrix, start_angle, ping_count):
    columns = focus_matrix.shape[1]
    sectors = raw_pings.shape[0]
    position = lax.axis_index("sector")
    received = lax.all_to_all(raw_pings, "sector", split_axis=0, concat_axis=1, tiled=True)[0]
    pings = received.shape[0]
    mask = (jnp.arange(pings, dtype=jnp.int32) < ping_count[position]).astype(jnp.bfloat16)
    angle = start_angle[position] - start_angle[(position + 1) % sectors]
    index = (angle * jnp.arange(columns, dtype=jnp.int32)) % columns
    phase = 2.0 * jnp.pi / columns * index.astype(jnp.float32)
    cosine, sine = jnp.cos(phase)[:, None], jnp.sin(phase)[:, None]
    h_real, h_imag = focus_matrix[0].astype(jnp.float32), focus_matrix[1].astype(jnp.float32)
    turned = jnp.stack([h_real * cosine - h_imag * sine, h_real * sine + h_imag * cosine]).astype(jnp.bfloat16)
    received, turned, mask = lax.optimization_barrier((received, turned, mask))
    own_pings = (received * mask[:, None, None]).reshape(pings, -1)
    other_pings = shifted(own_pings, "sector", -1)
    own, inverse, power = focus(focus_matrix, own_pings)
    coherence, interferogram = compare(turned, other_pings, own, inverse, power)
    return (coherence[None], interferogram[None])


def solution(mesh):
    return jax.shard_map(
        body,
        mesh=mesh,
        in_specs=(P("survey", "sector", None, None), P(), P("survey"), P("survey")),
        out_specs=(P(("survey", "sector"), None, None), P(("survey", "sector"), None, None, None)),
        check_vma=False,
    )
```

time: 138 us -> 120 us (0.87)
  Pallas kernels: 66.8 us -> 51.9 us
  waiting for transfers between devices: 45.3 us -> 37.1 us
  other arithmetic: 2.47 us -> 7.89 us
    pallas_call x1, Pallas kernels: 50.6 us -> 32.8 us  [compare(): pl.pallas_call(functools.partial(compare_kernel, chunks=chunks, rows=rows...]
    all_to_all x1, waiting for transfers between devices: 39.7 us -> 32.4 us  [body(): lax.all_to_all(raw_pings, 'sector', split_axis=0, concat_axis=1, tiled=True)]
    another operation x1 -> x2, other arithmetic: 0.02 us -> 5.31 us  [body(): jnp.stack([jnp.cos(phase), jnp.sin(phase)])[:, :, None]]
    pallas_call x1, Pallas kernels: 16.2 us -> 19.2 us  [focus(): pl.pallas_call(functools.partial(focus_kernel, chunks=chunks, rows=rows),...]
    broadcast_in_dim x1 -> x0, local copies, waits for them, and re-layouts: 1.91 us -> none  [body(): jnp.broadcast_to(jnp.stack([jnp.cos(phase), jnp.sin(phase)])[:, :, None],...]
  transfers between devices with their start and end apart: 2 -> 2, of which waited for: 2 -> 2; matrix products, arithmetic and copies ran while one was open for 2% -> 6% of each run, Pallas kernels for 12% -> 16%
where the time goes in v2:
time: 120 us; the launch traced here: 119 us
  Pallas kernels  51.9 us (43%)
  waiting for transfers between devices  37.1 us (31%)
  starting transfers between devices  17.4 us (14%)
  other arithmetic  7.89 us (7%)
  local copies, waits for them, and re-layouts  3.16 us (3%)
  between operations  2.01 us (2%)
    pallas_call x1, Pallas kernels, compare(): pl.pallas_call(functools.partial(compare_kernel, chunks=chunks, rows=rows...  32.8 us
    all_to_all x1, waiting for transfers between devices, body(): lax.all_to_all(raw_pings, 'sector', split_axis=0, concat_axis=1, tiled=True)  32.4 us
    pallas_call x1, Pallas kernels, focus(): pl.pallas_call(functools.partial(focus_kernel, chunks=chunks, rows=rows),...  19.2 us
    ppermute x1, starting transfers between devices, shifted(): return lax.ppermute(block, axis, route)  9.83 us
    all_to_all x1, starting transfers between devices, body(): lax.all_to_all(raw_pings, 'sector', split_axis=0, concat_axis=1, tiled=True)  7.56 us
    ppermute x1, waiting for transfers between devices, shifted(): return lax.ppermute(block, axis, route)  4.7 us
    another operation x1, other arithmetic  2.97 us
  transfers between devices with their start and end apart: 2, of which 2 were waited for; matrix products, arithmetic and copies ran while one was open for 6% of the time, Pallas kernels for 16%

profile of v2, /device:TPU:0, one launch (start us, length us, event | category | flops | bytes accessed | tf_op | source)
XLA Modules:
  0.0 119.5 jit_solution(12672353543661561999)
XLA Ops:
  0.6 0.0 copy-start.1
  0.6 0.0 copy-start
  0.6 7.6 %all-to-all-start = ((bf16[16,32,2,1024]{3,2,1,0:T(2,128)(2,1)}), bf16[16,32,2,1024]{3,2,1,0:T(2,128)(2,1)S(1)}, u32[]{:S(2)}, u32[]{:S(2)}) async-start(bf16[16,32,2,1024]{3,2,1,0:T(2,128)(2,1)} %param.4), calls=%async_computation | async-start | bytes 4194304 | tf_op jit(solution)/shard_map/all_to_all | solution.py:252
  8.2 0.0 copy-done.1
  8.2 0.6 dynamic_slice.11
  8.9 0.0 copy-done
  8.9 0.6 fusion.13
  10.8 0.6 fusion.12
  11.4 0.1 fusion.10
  11.5 3.0 %fusion.1 = (bf16[1,2048,512]{2,1,0:T(8,128)(2,1)S(1)}, bf16[1,2048,512]{2,1,0:T(8,128)(2,1)S(1)}) fusion(f32[2048]{0:T(1024)S(1)} %get-tuple-element.22, f32[2048]{0:T(1024)S(1)} %get-tuple-element.23, bf16[2,2048,512]{2,1,0:T(8,128)(2,1)} %h_ref.1), kind=kLoop, calls=%fused_computation.5 | loop fusion | flops 10485760 | bytes 8404992 | tf_op jit(solution)/shard_map/convert
  14.5 2.3 %pad_maximum_fusion.h_ref = bf16[2,2048,512]{2,1,0:T(8,128)(2,1)} fusion(bf16[1,2048,512]{2,1,0:T(8,128)(2,1)S(1)} %get-tuple-element.19, bf16[1,2048,512]{2,1,0:T(8,128)(2,1)S(1)} %get-tuple-element.18), kind=kLoop, calls=%fused_computation.8 | loop fusion | flops 2097152 | bytes 8388608 | tf_op jit(solution)/shard_map/stack | solution.py:260
  16.8 32.4 %all-to-all-done = bf16[16,32,2,1024]{3,2,1,0:T(2,128)(2,1)S(1)} async-done(((bf16[16,32,2,1024]{3,2,1,0:T(2,128)(2,1)}), bf16[16,32,2,1024]{3,2,1,0:T(2,128)(2,1)S(1)}, u32[]{:S(2)}, u32[]{:S(2)}) %all-to-all-start) | async-done | bytes 2097184 | tf_op jit(solution)/shard_map/all_to_all | solution.py:252
  49.2 1.9 %broadcast_multiply_fusion = bf16[512,2,1024]{2,1,0:T(2,128)(2,1)S(1)} fusion(bf16[512,2,1024]{2,1,0:T(2,128)(2,1)S(1)} %bitcast.7, bf16[512]{0:T(512)(128)(2,1)S(1)} %fusion.12), kind=kLoop, calls=%fused_computation.9 | loop fusion | flops 1048576 | bytes 4195328 | tf_op jit(solution)/shard_map/mul | solution.py:262
  51.1 1.9 %copy.6 = bf16[64,8,2,1024]{3,1,2,0:T(8,128)(2,1)} copy(bf16[64,8,2,1024]{3,2,1,0:T(2,128)(2,1)S(1)} %bitcast.8) | data formatting | bytes 4194304
  53.0 9.8 %collective-permute-start = (bf16[512,2048]{1,0:T(8,128)(2,1)}, bf16[512,2048]{1,0:T(8,128)(2,1)}, u32[]{:S(2)}, u32[]{:S(2)}) collective-permute-start(bf16[512,2048]{1,0:T(8,128)(2,1)} %bitcast.6.xr_ref.xi_ref), channel_id=1, source_target_pairs={{1,0},{2,1},{3,2},{4,3},{5,4},{6,5},{7,6},{8,7},{9,8},{10,9},{11,1... | collective-permute-start | bytes 6291464 | tf_op jit(solution)/shard_map/ppermute | solution.py:19
  62.9 19.2 %focus.1 = (f32[2,2048,1024]{2,1,0:T(8,128)}, f32[8,1024]{1,0:T(8,128)}, f32[2048,1024]{1,0:T(8,128)}) custom-call(bf16[2,2048,512]{2,1,0:T(8,128)(2,1)} %h_ref.1, bf16[512,2048]{1,0:T(8,128)(2,1)} %bitcast.6.xr_ref.xi_ref, bf16[512,2048]{1,0:T(8,128)(2,1)} %bitcast.6.xr_ref.xi_ref), custom_call_target="tpu_custom_call" | custom-call | flops 8589934592 | bytes 33554432 | tf_op jit(solution)/shard_map/focus/pallas_call | solution.py:125
  82.0 4.7 %collective-permute-done.xr_ref.xi_ref = bf16[512,2048]{1,0:T(8,128)(2,1)} collective-permute-done((bf16[512,2048]{1,0:T(8,128)(2,1)}, bf16[512,2048]{1,0:T(8,128)(2,1)}, u32[]{:S(2)}, u32[]{:S(2)}) %collective-permute-start) | collective-permute-done | bytes 2097184 | tf_op jit(solution)/shard_map/ppermute | solution.py:19
  86.7 32.8 %compare.8 = (f32[2048,1024]{1,0:T(8,128)}, bf16[2,2048,1024]{2,1,0:T(8,128)(2,1)}) custom-call(bf16[2,2048,512]{2,1,0:T(8,128)(2,1)} %pad_maximum_fusion.h_ref, bf16[512,2048]{1,0:T(8,128)(2,1)} %collective-permute-done.xr_ref.xi_ref, bf16[512,2048]{1,0:T(8,128)(2,1)} %collective-permute-done.xr_ref.xi_ref, f32[2,2048,1024]{2,1,0:T(8,128)} %get-tuple-element.13.f_ref, ...), custom_call_target="tpu_custom_call" | custom-call | tf_op jit(solution)/shard_map/compare/pallas_call | solution.py:216
Async XLA Ops:
  0.6 7.6 %copy-start.1 = (s32[16]{0:T(128)S(1)}, s32[16]{0:T(128)}, u32[]{:S(2)}) copy-start(s32[16]{0:T(128)} %param.7) | copy-start | bytes 196
  0.6 8.2 %copy-start = (s32[16]{0:T(128)S(1)}, s32[16]{0:T(128)}, u32[]{:S(2)}) copy-start(s32[16]{0:T(128)} %param.6) | copy-start | bytes 196
  0.6 48.5 %all-to-all-start = ((bf16[16,32,2,1024]{3,2,1,0:T(2,128)(2,1)}), bf16[16,32,2,1024]{3,2,1,0:T(2,128)(2,1)S(1)}, u32[]{:S(2)}, u32[]{:S(2)}) async-start(bf16[16,32,2,1024]{3,2,1,0:T(2,128)(2,1)} %param.4), calls=%async_computation | async-start | bytes 4194304 | tf_op jit(solution)/shard_map/all_to_all | solution.py:252
  53.0 33.7 %collective-permute-start = (bf16[512,2048]{1,0:T(8,128)(2,1)}, bf16[512,2048]{1,0:T(8,128)(2,1)}, u32[]{:S(2)}, u32[]{:S(2)}) collective-permute-start(bf16[512,2048]{1,0:T(8,128)(2,1)} %bitcast.6.xr_ref.xi_ref), channel_id=1, source_target_pairs={{1,0},{2,1},{3,2},{4,3},{5,4},{6,5},{7,6},{8,7},{9,8},{10,9},{11,1... | collective-permute-start | bytes 6291464 | tf_op jit(solution)/shard_map/ppermute | solution.py:19

commit v3 on v2

v3 whole, which is shorter than its diff:
```python
import functools

import jax
import jax.numpy as jnp
from jax import lax
from jax.experimental import pallas as pl
from jax.experimental.pallas import tpu as pltpu
from jax.sharding import PartitionSpec as P

WIN = 9
LANES = 128
CHUNK = 256
FOCUS_VMEM = 34 * 2**20
COMPARE_VMEM = 48 * 2**20
PART = 512


def shifted(block, axis, distance):
    devices = range(lax.axis_size(axis))
    route = [((i - distance) % len(devices), i) for i in devices]
    return lax.ppermute(block, axis, route)


def load_operand(count_ref, xr_ref, xi_ref, operand_ref):
    depth = xr_ref.shape[0]
    ping = lax.broadcasted_iota(jnp.int32, xr_ref.shape, 0)
    valid = jnp.where(ping < count_ref[0], 1.0, 0.0).astype(jnp.bfloat16)
    real, imag = xr_ref[...] * valid, xi_ref[...] * valid
    operand_ref[:depth, :CHUNK] = real
    operand_ref[:depth, CHUNK:] = imag
    operand_ref[depth:, :CHUNK] = -imag
    operand_ref[depth:, CHUNK:] = real


def band(weights_ref):
    size = weights_ref.shape[1]
    half = WIN // 2
    row = lax.broadcasted_iota(jnp.int32, (size, size), 0)
    column = lax.broadcasted_iota(jnp.int32, (size, size), 1)
    away = jnp.abs(row - column)
    plain = away <= half
    circular = plain | (away >= size - half)
    halves = plain & ((row < LANES) == (column < LANES))
    for index, kept in enumerate((plain, circular, halves)):
        weights_ref[index] = jnp.where(kept, 1.0, 0.0).astype(jnp.bfloat16)


def azimuth_windows(weights_ref, field_ref, looked_ref, tail_ref, step, scales):
    halo = 16
    size = weights_ref.shape[1]
    stride = size - 2 * halo
    columns = field_ref.shape[0]
    blocks = (columns - size) // stride + 1
    base = pl.multiple_of(step * CHUNK, CHUNK)
    for block in range(blocks):
        start = block * stride
        low = halo if block else 0
        high = size if block == blocks - 1 else size - halo
        here = pl.ds(start + low, high - low)
        total = jnp.dot(weights_ref[0], field_ref[pl.ds(start, size), :], preferred_element_type=jnp.float32)
        lane = lax.broadcasted_iota(jnp.int32, (high - low, LANES), 1)
        current = lane < LANES - (WIN - 1) * step
        for field, scale in enumerate(scales):
            scaled = total[low:high, field * CHUNK:(field + 1) * CHUNK] * scale
            last = scaled[:, LANES:]
            before = tail_ref[here, field * LANES:(field + 1) * LANES].astype(jnp.float32)
            looked_ref[field, here, pl.ds(base, LANES)] = scaled[:, :LANES].astype(jnp.bfloat16)
            looked_ref[field, here, pl.ds(base + LANES, LANES)] = jnp.where(current, last, before).astype(jnp.bfloat16)
            tail_ref[here, field * LANES:(field + 1) * LANES] = last.astype(jnp.bfloat16)


def range_windows(weights_ref, looked_ref, tail_ref, here, chunks):
    def product(operand, weights):
        return jnp.dot(operand, weights, preferred_element_type=jnp.float32)

    fields = looked_ref.shape[0]
    following = []
    for field in range(0, fields, 2):
        width = LANES * min(2, fields - field)
        edge = product(tail_ref[here, field * LANES:field * LANES + width], weights_ref[2, :width, :width])
        following += [edge[:, start:start + LANES] for start in range(0, width, LANES)]
    lane = lax.broadcasted_iota(jnp.int32, following[0].shape, 1)
    for chunk in reversed(range(chunks)):
        passes = [
            product(looked_ref[field, here, chunk * CHUNK:(chunk + 1) * CHUNK], weights_ref[1 if chunk else 0])
            for field in range(fields)
        ]
        current = lane < LANES - WIN // 2 - (WIN - 1) * chunk
        after = [jnp.where(current, value[:, LANES:], other) for value, other in zip(passes, following)]
        following = [value[:, LANES:] for value in passes]
        yield 2 * chunk + 1, after
        yield 2 * chunk, [value[:, :LANES] for value in passes]


def power_sum(power):
    return jnp.sum(power.reshape(power.shape[0] // 8, 8, power.shape[1]), axis=0)


def inverse_rms(sums, columns):
    return lax.rsqrt(jnp.sum(sums, axis=0, keepdims=True) / columns + 1e-06)


def focus_kernel(
    count_ref, h_ref, xr_ref, xi_ref, out_ref, inverse_ref, power_ref,
    operand_ref, field_ref, looked_ref, tail_ref, weights_ref, *, chunks, rows
):
    step = pl.program_id(0)
    columns = h_ref.shape[0]

    @pl.when(step == 0)
    def _():
        band(weights_ref)
        tail_ref[...] = jnp.zeros(tail_ref.shape, jnp.bfloat16)

    @pl.when(step < chunks)
    def _():
        load_operand(count_ref, xr_ref, xi_ref, operand_ref)

        def block_fields(block, sums):
            start = pl.multiple_of(block * rows, rows)
            here = pl.ds(start, rows)
            product = jnp.dot(h_ref[pl.ds(start, rows), :], operand_ref[...], preferred_element_type=jnp.float32)
            real, imag = product[:, :CHUNK], product[:, CHUNK:]
            out_ref[0, here, :] = real
            out_ref[1, here, :] = imag
            power = real * real + imag * imag
            field_ref[here, :] = power.astype(jnp.bfloat16)
            return sums + power_sum(power)

        sums = lax.fori_loop(0, columns // rows, block_fields, jnp.zeros((8, CHUNK), jnp.float32))
        inverse = inverse_rms(sums, columns)
        inverse_ref[...] = jnp.broadcast_to(inverse, inverse_ref.shape)
        azimuth_windows(weights_ref, field_ref, looked_ref, tail_ref, step, [inverse * inverse / (WIN * WIN)])

    @pl.when(step >= chunks)
    def _():
        size = power_ref.shape[0]
        here = pl.ds(pl.multiple_of((step - chunks) * size, size), size)
        for tile, (piece,) in range_windows(weights_ref, looked_ref, tail_ref, here, chunks):
            power_ref[:, tile * LANES:(tile + 1) * LANES] = piece.astype(power_ref.dtype)


def window_scratch(fields, columns, ranges, depth):
    return [
        pltpu.VMEM((2 * depth, 2 * CHUNK), jnp.bfloat16),
        pltpu.VMEM((columns, fields * CHUNK), jnp.bfloat16),
        pltpu.VMEM((fields, columns, ranges), jnp.bfloat16),
        pltpu.VMEM((columns, fields * LANES), jnp.bfloat16),
        pltpu.VMEM((3, CHUNK, CHUNK), jnp.bfloat16),
    ]


def focus(count, h, pings, rows=2048, out_rows=1024):
    columns, depth = h.shape[0], pings.shape[0]
    ranges = pings.shape[1] // 2
    chunks = ranges // CHUNK
    last = chunks - 1
    return pl.pallas_call(
        functools.partial(focus_kernel, chunks=chunks, rows=rows),
        grid=(chunks + columns // out_rows,),
        in_specs=[
            pl.BlockSpec(memory_space=pltpu.SMEM),
            pl.BlockSpec(h.shape, lambda j: (0, 0), pipeline_mode=pl.Buffered(1)),
            pl.BlockSpec((depth, CHUNK), lambda j: (0, jnp.minimum(j, last))),
            pl.BlockSpec((depth, CHUNK), lambda j: (0, chunks + jnp.minimum(j, last))),
        ],
        out_specs=[
            pl.BlockSpec((2, columns, CHUNK), lambda j: (0, 0, jnp.minimum(j, last))),
            pl.BlockSpec((8, CHUNK), lambda j: (0, jnp.minimum(j, last))),
            pl.BlockSpec((out_rows, ranges), lambda j: (jnp.maximum(j - chunks, 0), 0)),
        ],
        out_shape=[
            jax.ShapeDtypeStruct((2, columns, ranges), jnp.float32),
            jax.ShapeDtypeStruct((8, ranges), jnp.float32),
            jax.ShapeDtypeStruct((columns, ranges), jnp.bfloat16),
        ],
        scratch_shapes=window_scratch(1, columns, ranges, depth),
        compiler_params=pltpu.CompilerParams(vmem_limit_bytes=FOCUS_VMEM),
        cost_estimate=pl.CostEstimate(
            flops=8 * columns * depth * ranges, bytes_accessed=32 * 2**20, transcendentals=0
        ),
        name="focus",
    )(count, h, pings, pings)


def compare_kernel(
    count_ref, h_ref, xr_ref, xi_ref, f_ref, inverse_ref, power_ref, coherence_ref, interferogram_ref,
    operand_ref, field_ref, looked_ref, tail_ref, weights_ref, kept_ref, *, chunks, rows
):
    step = pl.program_id(0)
    columns = h_ref.shape[0]
    area = float(WIN * WIN)

    @pl.when(step == 0)
    def _():
        band(weights_ref)
        tail_ref[...] = jnp.zeros(tail_ref.shape, jnp.bfloat16)

    @pl.when(step < chunks)
    def _():
        load_operand(count_ref, xr_ref, xi_ref, operand_ref)

        def block_fields(block, sums):
            start = pl.multiple_of(block * rows, rows)
            product = jnp.dot(h_ref[pl.ds(start, rows), :], operand_ref[...], preferred_element_type=jnp.float32)
            here = pl.ds(start, rows)
            f_real, f_imag = f_ref[0, here, :], f_ref[1, here, :]
            g_real, g_imag = product[:, :CHUNK], product[:, CHUNK:]
            power = g_real * g_real + g_imag * g_imag
            field_ref[here, :CHUNK] = (f_real * g_real + f_imag * g_imag).astype(jnp.bfloat16)
            field_ref[here, CHUNK:2 * CHUNK] = (f_imag * g_real - f_real * g_imag).astype(jnp.bfloat16)
            field_ref[here, 2 * CHUNK:] = power.astype(jnp.bfloat16)
            return sums + power_sum(power)

        sums = lax.fori_loop(0, columns // rows, block_fields, jnp.zeros((8, CHUNK), jnp.float32))
        kept_ref[:, pl.ds(pl.multiple_of(step * CHUNK, CHUNK), CHUNK)] = power_ref[...]
        f_scale = inverse_ref[:1, :]
        g_scale = inverse_rms(sums, columns)
        cross = f_scale * g_scale / area
        scales = [cross, cross, g_scale * g_scale / area]
        azimuth_windows(weights_ref, field_ref, looked_ref, tail_ref, step, scales)

    @pl.when(step >= chunks)
    def _():
        size = coherence_ref.shape[0]
        part = min(size, PART)
        for first in range(0, size, part):
            here = pl.ds(pl.multiple_of((step - chunks) * size + first, part), part)
            rows_here = slice(first, first + part)
            for tile, values in range_windows(weights_ref, looked_ref, tail_ref, here, chunks):
                real, imag, g_power = values
                lanes = slice(tile * LANES, (tile + 1) * LANES)
                interferogram_ref[0, rows_here, lanes] = real.astype(jnp.bfloat16)
                interferogram_ref[1, rows_here, lanes] = imag.astype(jnp.bfloat16)
                power = real * real + imag * imag
                energy = kept_ref[here, lanes].astype(jnp.float32) * g_power + 1e-06 / (area * area)
                coherence_ref[rows_here, lanes] = power * lax.rsqrt(jnp.maximum(power * energy, 1e-37))


def compare(count, h, pings, own, inverse, power, rows=1024, out_rows=512):
    columns, depth = h.shape[0], pings.shape[0]
    ranges = pings.shape[1] // 2
    chunks = ranges // CHUNK
    last = chunks - 1
    return pl.pallas_call(
        functools.partial(compare_kernel, chunks=chunks, rows=rows),
        grid=(chunks + columns // out_rows,),
        in_specs=[
            pl.BlockSpec(memory_space=pltpu.SMEM),
            pl.BlockSpec(h.shape, lambda j: (0, 0), pipeline_mode=pl.Buffered(1)),
            pl.BlockSpec((depth, CHUNK), lambda j: (0, jnp.minimum(j, last))),
            pl.BlockSpec((depth, CHUNK), lambda j: (0, chunks + jnp.minimum(j, last))),
            pl.BlockSpec((2, columns, CHUNK), lambda j: (0, 0, jnp.minimum(j, last))),
            pl.BlockSpec((8, CHUNK), lambda j: (0, jnp.minimum(j, last))),
            pl.BlockSpec((columns, CHUNK), lambda j: (0, jnp.minimum(j, last))),
        ],
        out_specs=[
            pl.BlockSpec((out_rows, ranges), lambda j: (jnp.maximum(j - chunks, 0), 0)),
            pl.BlockSpec((2, out_rows, ranges), lambda j: (0, jnp.maximum(j - chunks, 0), 0)),
        ],
        out_shape=[
            jax.ShapeDtypeStruct((columns, ranges), jnp.float32),
            jax.ShapeDtypeStruct((2, columns, ranges), jnp.bfloat16),
        ],
        scratch_shapes=window_scratch(3, columns, ranges, depth) + [pltpu.VMEM((columns, ranges), jnp.bfloat16)],
        compiler_params=pltpu.CompilerParams(vmem_limit_bytes=COMPARE_VMEM),
        name="compare",
    )(count, h, pings, pings, own, inverse, power)


def body(raw_pings, focus_matrix, start_angle, ping_count):
    columns = focus_matrix.shape[1]
    sectors = raw_pings.shape[0]
    position = lax.axis_index("sector")
    neighbour = (position + 1) % sectors
    received = lax.all_to_all(raw_pings, "sector", split_axis=0, concat_axis=1, tiled=True)[0]
    angle = start_angle[position] - start_angle[neighbour]
    index = (angle * jnp.arange(columns, dtype=jnp.int32)) % columns
    phase = 2.0 * jnp.pi / columns * index.astype(jnp.float32)
    cosine, sine = jnp.cos(phase)[:, None], jnp.sin(phase)[:, None]
    h_real, h_imag = focus_matrix[0].astype(jnp.float32), focus_matrix[1].astype(jnp.float32)
    turned = [h_real * cosine - h_imag * sine, h_real * sine + h_imag * cosine]
    turned = jnp.concatenate([part.astype(jnp.bfloat16) for part in turned], axis=1)
    plain = jnp.concatenate([focus_matrix[0], focus_matrix[1]], axis=1)
    counts = ping_count[jnp.stack([position, neighbour])]
    received, plain, turned, counts = lax.optimization_barrier((received, plain, turned, counts))
    own_pings = received.reshape(received.shape[0], -1)
    other_pings = shifted(own_pings, "sector", -1)
    own, inverse, power = focus(counts[:1], plain, own_pings)
    coherence, interferogram = compare(counts[1:], turned, other_pings, own, inverse, power)
    return (coherence[None], interferogram[None])


def solution(mesh):
    return jax.shard_map(
        body,
        mesh=mesh,
        in_specs=(P("survey", "sector", None, None), P(), P("survey"), P("survey")),
        out_specs=(P(("survey", "sector"), None, None), P(("survey", "sector"), None, None, None)),
        check_vma=False,
    )
```

time: 120 us -> 117 us (0.975)
  waiting for transfers between devices: 37.1 us -> 32.9 us
  local copies, waits for them, and re-layouts: 3.16 us -> 5.58 us
  Pallas kernels: 51.9 us -> 50.1 us
    concatenate x0 -> x2, other arithmetic: none -> 5.44 us  [the longest x1 2.76 us: body(): jnp.concatenate([part.astype(jnp.bfloat16) for part in turned], axis=1)]
    another operation x2 -> x0, other arithmetic: 5.31 us -> none
    all_to_all x1, waiting for transfers between devices: 32.4 us -> 28.7 us  [body(): lax.all_to_all(raw_pings, 'sector', split_axis=0, concat_axis=1, tiled=True)]
    pallas_call x1, Pallas kernels: 19.2 us -> 16.8 us  [focus(): pl.pallas_call(functools.partial(focus_kernel, chunks=chunks, rows=rows),...]
    convert_element_type x1, other arithmetic: 0.63 us -> 2.97 us  [body(): part.astype(jnp.bfloat16)]
    mul x1 -> x0, other arithmetic: 1.89 us -> none  [body(): own_pings = (received * mask[:, None, None]).reshape(pings, -1)]
    unnamed x5 -> x13, local copies, waits for them, and re-layouts: 1.94 us -> 3.45 us
  transfers between devices with their start and end apart: 2 -> 2, of which waited for: 2 -> 2; matrix products, arithmetic and copies ran while one was open for 6% -> 9% of each run, Pallas kernels for 16% -> 14%
where the time goes in v3:
time: 117 us
  Pallas kernels  50.1 us (43%)
  waiting for transfers between devices  32.9 us (28%)
  starting transfers between devices  17.4 us (15%)
  other arithmetic  8.56 us (7%)
  local copies, waits for them, and re-layouts  5.58 us (5%)
  between operations  1.98 us (2%)
    pallas_call x1, Pallas kernels, compare(): pl.pallas_call(functools.partial(compare_kernel, chunks=chunks, rows=rows...  33.3 us
    all_to_all x1, waiting for transfers between devices, body(): lax.all_to_all(raw_pings, 'sector', split_axis=0, concat_axis=1, tiled=True)  28.7 us
    pallas_call x1, Pallas kernels, focus(): pl.pallas_call(functools.partial(focus_kernel, chunks=chunks, rows=rows),...  16.8 us
    ppermute x1, starting transfers between devices, shifted(): return lax.ppermute(block, axis, route)  9.89 us
    all_to_all x1, starting transfers between devices, body(): lax.all_to_all(raw_pings, 'sector', split_axis=0, concat_axis=1, tiled=True)  7.56 us
    ppermute x1, waiting for transfers between devices, shifted(): return lax.ppermute(block, axis, route)  4.25 us
    unnamed x13, local copies, waits for them, and re-layouts  3.45 us
    convert_element_type x1, other arithmetic, body(): part.astype(jnp.bfloat16)  2.97 us
  transfers between devices with their start and end apart: 2, of which 2 were waited for; matrix products, arithmetic and copies ran while one was open for 9% of the time, Pallas kernels for 14%

profile of v3, /device:TPU:0, one launch (start us, length us, event | category | flops | bytes accessed | tf_op | source)
XLA Modules:
  0.0 116.6 jit_solution(12896142064726857629)
XLA Ops:
  0.6 0.0 copy-start
  0.6 0.0 copy-start.5
  0.7 7.6 %all-to-all-start = ((bf16[16,32,2,1024]{3,2,1,0:T(2,128)(2,1)}), bf16[16,32,2,1024]{3,2,1,0:T(2,128)(2,1)S(1)}, u32[]{:S(2)}, u32[]{:S(2)}) async-start(bf16[16,32,2,1024]{3,2,1,0:T(2,128)(2,1)} %param.4), calls=%async_computation | async-start | bytes 4194304 | tf_op jit(solution)/shard_map/all_to_all | solution.py:276
  8.2 0.0 copy-done.5
  8.2 0.7 fusion.14
  10.2 0.1 fusion.12
  10.2 0.0 copy-done
  10.3 0.6 gather_fusion
  10.9 0.1 fusion.10
  11.0 3.0 %fusion.1 = (bf16[2048,512]{1,0:T(8,128)(2,1)S(1)}, bf16[2048,512]{1,0:T(8,128)(2,1)S(1)}) fusion(f32[2048]{0:T(1024)S(1)} %get-tuple-element.28, f32[2048]{0:T(1024)S(1)} %get-tuple-element.29, bf16[2,2048,512]{2,1,0:T(8,128)(2,1)} %param.5), kind=kLoop, calls=%fused_computation.6 | loop fusion | flops 10485760 | bytes 8404992 | tf_op jit(solution)/shard_map/convert_element_type | solution.py:283
  13.9 0.0 copy-start.4
  13.9 2.8 %pad_maximum_fusion.1.h_ref = bf16[2048,1024]{1,0:T(8,128)(2,1)} fusion(bf16[2048,512]{1,0:T(8,128)(2,1)S(1)} %get-tuple-element.21, bf16[2048,512]{1,0:T(8,128)(2,1)S(1)} %get-tuple-element.20), kind=kLoop, calls=%fused_computation.10 | loop fusion | flops 8388608 | bytes 8388608 | tf_op jit(solution)/shard_map/concatenate | solution.py:283
  16.7 0.9 copy-done.4
  17.6 0.3 slice_bitcast_fusion.1
  17.8 2.7 %pad_maximum_fusion.h_ref = bf16[2048,1024]{1,0:T(8,128)(2,1)} fusion(bf16[2048,512]{1,0:T(8,128)(2,1)S(1)} %get-tuple-element.23, bf16[2048,512]{1,0:T(8,128)(2,1)S(1)} %get-tuple-element.22), kind=kLoop, calls=%fused_computation.9 | loop fusion | flops 8388608 | bytes 8388608 | tf_op jit(solution)/shard_map/concatenate | solution.py:284
  20.5 28.7 %all-to-all-done = bf16[16,32,2,1024]{3,2,1,0:T(2,128)(2,1)S(1)} async-done(((bf16[16,32,2,1024]{3,2,1,0:T(2,128)(2,1)}), bf16[16,32,2,1024]{3,2,1,0:T(2,128)(2,1)S(1)}, u32[]{:S(2)}, u32[]{:S(2)}) %all-to-all-start) | async-done | bytes 2097184 | tf_op jit(solution)/shard_map/all_to_all | solution.py:276
  49.2 0.6 copy.6
  49.8 9.9 %collective-permute-start = (bf16[512,2048]{1,0:T(8,128)(2,1)S(1)}, bf16[512,2048]{1,0:T(8,128)(2,1)S(1)}, u32[]{:S(2)}, u32[]{:S(2)}) collective-permute-start(bf16[512,2048]{1,0:T(8,128)(2,1)S(1)} %bitcast.22), channel_id=1, source_target_pairs={{1,0},{2,1},{3,2},{4,3},{5,4},{6,5},{7,6},{8,7},{9,8},{10,9},{11,1... | collective-permute-start | bytes 6291464 | tf_op jit(solution)/shard_map/ppermute | solution.py:21
  59.7 0.6 fusion.13
  60.3 16.8 %focus.1 = (f32[2,2048,1024]{2,1,0:T(8,128)}, f32[8,1024]{1,0:T(8,128)S(1)}, bf16[2048,1024]{1,0:T(8,128)(2,1)S(1)}) custom-call(s32[1]{0:T(128)} %get-tuple-element.24.count_ref, bf16[2048,1024]{1,0:T(8,128)(2,1)S(1)} %copy-done.3, bf16[512,2048]{1,0:T(8,128)(2,1)S(1)} %bitcast.23, bf16[512,2048]{1,0:T(8,128)(2,1)S(1)} %bitcast.24), custom_call_target="tpu_custom_call" | custom-call | flops 8589934592 | bytes 33554432 | tf_op jit(solution)/shard_map/focus/pallas_call | solution.py:158
  77.0 2.0 %copy-done.2 = bf16[2048,1024]{1,0:T(8,128)(2,1)} copy-done((bf16[2048,1024]{1,0:T(8,128)(2,1)}, bf16[2048,1024]{1,0:T(8,128)(2,1)S(1)}, u32[]{:S(2)}) %copy-start.2) | copy-done | bytes 4194328
  79.0 4.3 %collective-permute-done.xr_ref.xi_ref = bf16[512,2048]{1,0:T(8,128)(2,1)S(1)} collective-permute-done((bf16[512,2048]{1,0:T(8,128)(2,1)S(1)}, bf16[512,2048]{1,0:T(8,128)(2,1)S(1)}, u32[]{:S(2)}, u32[]{:S(2)}) %collective-permute-start) | collective-permute-done | bytes 2097184 | tf_op jit(solution)/shard_map/ppermute | solution.py:21
  83.2 33.3 %compare.8 = (f32[2048,1024]{1,0:T(8,128)}, bf16[2,2048,1024]{2,1,0:T(8,128)(2,1)}) custom-call(s32[1]{0:T(128)} %get-tuple-element.25.count_ref, bf16[2048,1024]{1,0:T(8,128)(2,1)} %pad_maximum_fusion.1.h_ref, bf16[512,2048]{1,0:T(8,128)(2,1)S(1)} %collective-permute-done.xr_ref.xi_ref, bf16[512,2048]{1,0:T(8,128)(2,1)S(1)} %collective-permute-done.xr_ref.xi_ref, ...), custom_call_target="tpu_custom_call" | custom-call | tf_op jit(solution)/shard_map/compare/pallas_call | solution.py:245
  116.6 0.0 copy-done.1
  (5 shorter events, 0.0 us)
Async XLA Ops:
  0.6 9.6 %copy-start = (s32[16]{0:T(128)S(1)}, s32[16]{0:T(128)}, u32[]{:S(2)}) copy-start(s32[16]{0:T(128)} %param.7) | copy-start | bytes 196
  0.6 7.6 %copy-start.5 = (s32[16]{0:T(128)S(1)}, s32[16]{0:T(128)}, u32[]{:S(2)}) copy-start(s32[16]{0:T(128)} %param.6) | copy-start | bytes 196
  0.7 48.5 %all-to-all-start = ((bf16[16,32,2,1024]{3,2,1,0:T(2,128)(2,1)}), bf16[16,32,2,1024]{3,2,1,0:T(2,128)(2,1)S(1)}, u32[]{:S(2)}, u32[]{:S(2)}) async-start(bf16[16,32,2,1024]{3,2,1,0:T(2,128)(2,1)} %param.4), calls=%async_computation | async-start | bytes 4194304 | tf_op jit(solution)/shard_map/all_to_all | solution.py:276
  13.9 3.6 %copy-start.4 = (bf16[2,2048,512]{2,1,0:T(8,128)(2,1)S(1)}, bf16[2,2048,512]{2,1,0:T(8,128)(2,1)}, u32[]{:S(2)}) copy-start(bf16[2,2048,512]{2,1,0:T(8,128)(2,1)} %param.5) | copy-start | bytes 12582916
  49.2 11.1 %copy-start.3 = (bf16[2048,1024]{1,0:T(8,128)(2,1)S(1)}, bf16[2048,1024]{1,0:T(8,128)(2,1)}, u32[]{:S(2)}) copy-start(bf16[2048,1024]{1,0:T(8,128)(2,1)} %pad_maximum_fusion.h_ref) | copy-start | bytes 12582916
  49.8 33.4 %collective-permute-start = (bf16[512,2048]{1,0:T(8,128)(2,1)S(1)}, bf16[512,2048]{1,0:T(8,128)(2,1)S(1)}, u32[]{:S(2)}, u32[]{:S(2)}) collective-permute-start(bf16[512,2048]{1,0:T(8,128)(2,1)S(1)} %bitcast.22), channel_id=1, source_target_pairs={{1,0},{2,1},{3,2},{4,3},{5,4},{6,5},{7,6},{8,7},{9,8},{10,9},{11,1... | collective-permute-start | bytes 6291464 | tf_op jit(solution)/shard_map/ppermute | solution.py:21
  77.0 2.0 %copy-start.2 = (bf16[2048,1024]{1,0:T(8,128)(2,1)}, bf16[2048,1024]{1,0:T(8,128)(2,1)S(1)}, u32[]{:S(2)}) copy-start(bf16[2048,1024]{1,0:T(8,128)(2,1)S(1)} %get-tuple-element.17.power_ref) | copy-start | bytes 12582916
  83.2 33.3 %copy-start.1 = (s32[16]{0:T(128)S(1)}, s32[16]{0:T(128)}, u32[]{:S(2)}) copy-start(s32[16]{0:T(128)} %param.7) | copy-start | bytes 196

commit v4 on v3

--- a/solution.py
+++ b/solution.py
@@ -11,7 +11,9 @@
 LANES = 128
 CHUNK = 256
 FOCUS_VMEM = 34 * 2**20
-COMPARE_VMEM = 48 * 2**20
+FIRST_VMEM = 32 * 2**20
+PIECES = 2
+COMPARE_VMEM = 44 * 2**20
 PART = 512
 
 
@@ -45,13 +47,12 @@
         weights_ref[index] = jnp.where(kept, 1.0, 0.0).astype(jnp.bfloat16)
 
 
-def azimuth_windows(weights_ref, field_ref, looked_ref, tail_ref, step, scales):
+def azimuth_windows(weights_ref, field_ref, looked_ref, tail_ref, base, step, scales):
     halo = 16
     size = weights_ref.shape[1]
     stride = size - 2 * halo
     columns = field_ref.shape[0]
     blocks = (columns - size) // stride + 1
-    base = pl.multiple_of(step * CHUNK, CHUNK)
     for block in range(blocks):
         start = block * stride
         low = halo if block else 0
@@ -101,9 +102,10 @@
 
 
 def focus_kernel(
-    count_ref, h_ref, xr_ref, xi_ref, out_ref, inverse_ref, power_ref,
-    operand_ref, field_ref, looked_ref, tail_ref, weights_ref, *, chunks, rows
+    count_ref, h_ref, *refs, chunks, rows
 ):
+    pieces = refs[:-8]
+    out_ref, inverse_ref, power_ref, operand_ref, field_ref, looked_ref, tail_ref, weights_ref = refs[-8:]
     step = pl.program_id(0)
     columns = h_ref.shape[0]
 
@@ -112,10 +114,14 @@
         band(weights_ref)
         tail_ref[...] = jnp.zeros(tail_ref.shape, jnp.bfloat16)
 
+    each = chunks // (len(pieces) // 2)
+    for piece in range(len(pieces) // 2):
+        @pl.when(step // each == piece)
+        def _():
+            load_operand(count_ref, pieces[2 * piece], pieces[2 * piece + 1], operand_ref)
+
     @pl.when(step < chunks)
     def _():
-        load_operand(count_ref, xr_ref, xi_ref, operand_ref)
-
         def block_fields(block, sums):
             start = pl.multiple_of(block * rows, rows)
             here = pl.ds(start, rows)
@@ -130,7 +136,8 @@
         sums = lax.fori_loop(0, columns // rows, block_fields, jnp.zeros((8, CHUNK), jnp.float32))
         inverse = inverse_rms(sums, columns)
         inverse_ref[...] = jnp.broadcast_to(inverse, inverse_ref.shape)
-        azimuth_windows(weights_ref, field_ref, looked_ref, tail_ref, step, [inverse * inverse / (WIN * WIN)])
+        base = pl.multiple_of(step * CHUNK, CHUNK)
+        azimuth_windows(weights_ref, field_ref, looked_ref, tail_ref, base, step, [inverse * inverse / (WIN * WIN)])
 
     @pl.when(step >= chunks)
     def _():
@@ -151,19 +158,22 @@
 
 
 def focus(count, h, pings, rows=2048, out_rows=1024):
-    columns, depth = h.shape[0], pings.shape[0]
-    ranges = pings.shape[1] // 2
-    chunks = ranges // CHUNK
+    columns, depth = h.shape[0], pings[0].shape[0]
+    each = pings[0].shape[1] // 2 // CHUNK
+    chunks = each * len(pings)
+    ranges = chunks * CHUNK
     last = chunks - 1
+
+    def ping_spec(piece, half):
+        return pl.BlockSpec((depth, CHUNK), lambda j: (0, half * each + jnp.clip(j - piece * each, 0, each - 1)))
+
     return pl.pallas_call(
         functools.partial(focus_kernel, chunks=chunks, rows=rows),
         grid=(chunks + columns // out_rows,),
         in_specs=[
             pl.BlockSpec(memory_space=pltpu.SMEM),
             pl.BlockSpec(h.shape, lambda j: (0, 0), pipeline_mode=pl.Buffered(1)),
-            pl.BlockSpec((depth, CHUNK), lambda j: (0, jnp.minimum(j, last))),
-            pl.BlockSpec((depth, CHUNK), lambda j: (0, chunks + jnp.minimum(j, last))),
-        ],
+        ] + [ping_spec(piece, half) for piece in range(len(pings)) for half in range(2)],
         out_specs=[
             pl.BlockSpec((2, columns, CHUNK), lambda j: (0, 0, jnp.minimum(j, last))),
             pl.BlockSpec((8, CHUNK), lambda j: (0, jnp.minimum(j, last))),
@@ -180,92 +190,180 @@
             flops=8 * columns * depth * ranges, bytes_accessed=32 * 2**20, transcendentals=0
         ),
         name="focus",
-    )(count, h, pings, pings)
-
-
-def compare_kernel(
-    count_ref, h_ref, xr_ref, xi_ref, f_ref, inverse_ref, power_ref, coherence_ref, interferogram_ref,
-    operand_ref, field_ref, looked_ref, tail_ref, weights_ref, kept_ref, *, chunks, rows
+    )(count, h, *[array for array in pings for _ in range(2)])
+
+
+def cross_windows(
+    count_ref, h_ref, xr_ref, xi_ref, f_ref, inverse_ref, operand_ref, field_ref, looked_ref, tail_ref, weights_ref,
+    base, chunk, rows, before=None
+):
+    columns = h_ref.shape[0]
+    area = float(WIN * WIN)
+    load_operand(count_ref, xr_ref, xi_ref, operand_ref)
+
+    def block_fields(block, sums):
+        start = pl.multiple_of(block * rows, rows)
+        product = jnp.dot(h_ref[pl.ds(start, rows), :], operand_ref[...], preferred_element_type=jnp.float32)
+        here = pl.ds(start, rows)
+        f_real, f_imag = f_ref[0, here, :], f_ref[1, here, :]
+        g_real, g_imag = product[:, :CHUNK], product[:, CHUNK:]
+        power = g_real * g_real + g_imag * g_imag
+        field_ref[here, :CHUNK] = (f_real * g_real + f_imag * g_imag).astype(jnp.bfloat16)
+        field_ref[here, CHUNK:2 * CHUNK] = (f_imag * g_real - f_real * g_imag).astype(jnp.bfloat16)
+        field_ref[here, 2 * CHUNK:] = power.astype(jnp.bfloat16)
+        return sums + power_sum(power)
+
+    sums = lax.fori_loop(0, columns // rows, block_fields, jnp.zeros((8, CHUNK), jnp.float32))
+    f_scale = inverse_ref[:1, :]
+    g_scale = inverse_rms(sums, columns)
+    cross = f_scale * g_scale / area
+    if before is not None:
+        before()
+    scales = [cross, cross, g_scale * g_scale / area]
+    azimuth_windows(weights_ref, field_ref, looked_ref, tail_ref, base, chunk, scales)
+
+
+def first_kernel(
+    count_ref, h_ref, xr_ref, xi_ref, f_ref, inverse_ref, looked_ref, tail_ref, operand_ref, field_ref, weights_ref,
+    *, rows
 ):
     step = pl.program_id(0)
-    columns = h_ref.shape[0]
-    area = float(WIN * WIN)
 
     @pl.when(step == 0)
     def _():
         band(weights_ref)
         tail_ref[...] = jnp.zeros(tail_ref.shape, jnp.bfloat16)
 
-    @pl.when(step < chunks)
-    def _():
-        load_operand(count_ref, xr_ref, xi_ref, operand_ref)
-
-        def block_fields(block, sums):
-            start = pl.multiple_of(block * rows, rows)
-            product = jnp.dot(h_ref[pl.ds(start, rows), :], operand_ref[...], preferred_element_type=jnp.float32)
-            here = pl.ds(start, rows)
-            f_real, f_imag = f_ref[0, here, :], f_ref[1, here, :]
-            g_real, g_imag = product[:, :CHUNK], product[:, CHUNK:]
-            power = g_real * g_real + g_imag * g_imag
-            field_ref[here, :CHUNK] = (f_real * g_real + f_imag * g_imag).astype(jnp.bfloat16)
-            field_ref[here, CHUNK:2 * CHUNK] = (f_imag * g_real - f_real * g_imag).astype(jnp.bfloat16)
-            field_ref[here, 2 * CHUNK:] = power.astype(jnp.bfloat16)
-            return sums + power_sum(power)
-
-        sums = lax.fori_loop(0, columns // rows, block_fields, jnp.zeros((8, CHUNK), jnp.float32))
-        kept_ref[:, pl.ds(pl.multiple_of(step * CHUNK, CHUNK), CHUNK)] = power_ref[...]
-        f_scale = inverse_ref[:1, :]
-        g_scale = inverse_rms(sums, columns)
-        cross = f_scale * g_scale / area
-        scales = [cross, cross, g_scale * g_scale / area]
-        azimuth_windows(weights_ref, field_ref, looked_ref, tail_ref, step, scales)
-
-    @pl.when(step >= chunks)
+    cross_windows(
+        count_ref, h_ref, xr_ref, xi_ref, f_ref, inverse_ref,
+        operand_ref, field_ref, looked_ref, tail_ref, weights_ref, 0, step, rows
+    )
+
+
+def compare_first(count, h, pings, own, inverse, rows=1024):
+    columns, depth = h.shape[0], pings.shape[0]
+    chunks = pings.shape[1] // 2 // CHUNK
+    fields = 3
+    return pl.pallas_call(
+        functools.partial(first_kernel, rows=rows),
+        grid=(chunks,),
+        in_specs=[
+            pl.BlockSpec(memory_space=pltpu.SMEM),
+            pl.BlockSpec(h.shape, lambda j: (0, 0), pipeline_mode=pl.Buffered(1)),
+            pl.BlockSpec((depth, CHUNK), lambda j: (0, j)),
+            pl.BlockSpec((depth, CHUNK), lambda j: (0, chunks + j)),
+            pl.BlockSpec((2, columns, CHUNK), lambda j: (0, 0, j)),
+            pl.BlockSpec((8, CHUNK), lambda j: (0, j)),
+        ],
+        out_specs=[
+            pl.BlockSpec((fields, columns, CHUNK), lambda j: (0, 0, j)),
+            pl.BlockSpec((columns, fields * LANES), lambda j: (0, 0)),
+        ],
+        out_shape=[
+            pltpu.HBM((fields, columns, chunks * CHUNK), jnp.bfloat16),
+            jax.ShapeDtypeStruct((columns, fields * LANES), jnp.bfloat16),
+        ],
+        scratch_shapes=[
+            pltpu.VMEM((2 * depth, 2 * CHUNK), jnp.bfloat16),
+            pltpu.VMEM((columns, fields * CHUNK), jnp.bfloat16),
+            pltpu.VMEM((3, CHUNK, CHUNK), jnp.bfloat16),
+        ],
+        compiler_params=pltpu.CompilerParams(vmem_limit_bytes=FIRST_VMEM),
+        cost_estimate=pl.CostEstimate(
+            flops=8 * columns * depth * chunks * CHUNK, bytes_accessed=24 * 2**20, transcendentals=0
+        ),
+        name="compare_first",
+    )(count, h, pings, pings, own, inverse)
+
+
+def compare_kernel(
+    count_ref, h_ref, xr_ref, xi_ref, f_ref, inverse_ref, power_ref, begun_ref, edge_ref,
+    coherence_ref, interferogram_ref,
+    operand_ref, field_ref, looked_ref, tail_ref, weights_ref, kept_ref, sems, *, first, chunks, rows
+):
+    step = pl.program_id(0)
+    area = float(WIN * WIN)
+    fresh = chunks - first
+    edge_copy = pltpu.make_async_copy(edge_ref, tail_ref, sems.at[0])
+    begun_copy = pltpu.make_async_copy(begun_ref, looked_ref.at[:, :, pl.ds(0, first * CHUNK)], sems.at[1])
+    power_copy = pltpu.make_async_copy(power_ref, kept_ref, sems.at[2])
+
+    @pl.when(step == 0)
+    def _():
+        edge_copy.start()
+        begun_copy.start()
+        power_copy.start()
+        band(weights_ref)
+
+    def wait_edge():
+        @pl.when(step == 0)
+        def _():
+            edge_copy.wait()
+
+    @pl.when(step < fresh)
+    def _():
+        chunk = first + step
+        cross_windows(
+            count_ref, h_ref, xr_ref, xi_ref, f_ref, inverse_ref,
+            operand_ref, field_ref, looked_ref, tail_ref, weights_ref,
+            pl.multiple_of(chunk * CHUNK, CHUNK), chunk, rows, wait_edge
+        )
+
+    @pl.when(step == fresh)
+    def _():
+        begun_copy.wait()
+        power_copy.wait()
+
+    @pl.when(step >= fresh)
     def _():
         size = coherence_ref.shape[0]
-        part = min(size, PART)
-        for first in range(0, size, part):
-            here = pl.ds(pl.multiple_of((step - chunks) * size + first, part), part)
-            rows_here = slice(first, first + part)
-            for tile, values in range_windows(weights_ref, looked_ref, tail_ref, here, chunks):
-                real, imag, g_power = values
-                lanes = slice(tile * LANES, (tile + 1) * LANES)
-                interferogram_ref[0, rows_here, lanes] = real.astype(jnp.bfloat16)
-                interferogram_ref[1, rows_here, lanes] = imag.astype(jnp.bfloat16)
-                power = real * real + imag * imag
-                energy = kept_ref[here, lanes].astype(jnp.float32) * g_power + 1e-06 / (area * area)
-                coherence_ref[rows_here, lanes] = power * lax.rsqrt(jnp.maximum(power * energy, 1e-37))
-
-
-def compare(count, h, pings, own, inverse, power, rows=1024, out_rows=512):
+        here = pl.ds(pl.multiple_of((step - fresh) * size, size), size)
+        for tile, values in range_windows(weights_ref, looked_ref, tail_ref, here, chunks):
+            real, imag, g_power = values
+            lanes = slice(tile * LANES, (tile + 1) * LANES)
+            interferogram_ref[0, :, lanes] = real.astype(jnp.bfloat16)
+            interferogram_ref[1, :, lanes] = imag.astype(jnp.bfloat16)
+            power = real * real + imag * imag
+            energy = kept_ref[here, lanes].astype(jnp.float32) * g_power + 1e-06 / (area * area)
+            coherence_ref[:, lanes] = power * lax.rsqrt(jnp.maximum(power * energy, 1e-37))
+
+
+def compare(count, h, pings, own, inverse, power, begun, edge, rows=1024, out_rows=512):
     columns, depth = h.shape[0], pings.shape[0]
-    ranges = pings.shape[1] // 2
+    ranges = power.shape[1]
     chunks = ranges // CHUNK
-    last = chunks - 1
+    first = begun.shape[2] // CHUNK
+    fresh = chunks - first
+    last = fresh - 1
     return pl.pallas_call(
-        functools.partial(compare_kernel, chunks=chunks, rows=rows),
-        grid=(chunks + columns // out_rows,),
+        functools.partial(compare_kernel, first=first, chunks=chunks, rows=rows),
+        grid=(fresh + columns // out_rows,),
         in_specs=[
             pl.BlockSpec(memory_space=pltpu.SMEM),
             pl.BlockSpec(h.shape, lambda j: (0, 0), pipeline_mode=pl.Buffered(1)),
             pl.BlockSpec((depth, CHUNK), lambda j: (0, jnp.minimum(j, last))),
-            pl.BlockSpec((depth, CHUNK), lambda j: (0, chunks + jnp.minimum(j, last))),
-            pl.BlockSpec((2, columns, CHUNK), lambda j: (0, 0, jnp.minimum(j, last))),
-            pl.BlockSpec((8, CHUNK), lambda j: (0, jnp.minimum(j, last))),
-            pl.BlockSpec((columns, CHUNK), lambda j: (0, jnp.minimum(j, last))),
-        ],
+            pl.BlockSpec((depth, CHUNK), lambda j: (0, fresh + jnp.minimum(j, last))),
+            pl.BlockSpec((2, columns, CHUNK), lambda j: (0, 0, first + jnp.minimum(j, last))),
+            pl.BlockSpec((8, CHUNK), lambda j: (0, first + jnp.minimum(j, last))),
+        ] + [pl.BlockSpec(memory_space=pl.ANY)] * 3,
         out_specs=[
-            pl.BlockSpec((out_rows, ranges), lambda j: (jnp.maximum(j - chunks, 0), 0)),
-            pl.BlockSpec((2, out_rows, ranges), lambda j: (0, jnp.maximum(j - chunks, 0), 0)),
+            pl.BlockSpec((out_rows, ranges), lambda j: (jnp.maximum(j - fresh, 0), 0)),
+            pl.BlockSpec((2, out_rows, ranges), lambda j: (0, jnp.maximum(j - fresh, 0), 0)),
         ],
         out_shape=[
             jax.ShapeDtypeStruct((columns, ranges), jnp.float32),
             jax.ShapeDtypeStruct((2, columns, ranges), jnp.bfloat16),
         ],
-        scratch_shapes=window_scratch(3, columns, ranges, depth) + [pltpu.VMEM((columns, ranges), jnp.bfloat16)],
+        scratch_shapes=window_scratch(3, columns, ranges, depth) + [
+            pltpu.VMEM((columns, ranges), jnp.bfloat16),
+            pltpu.SemaphoreType.DMA((3,)),
+        ],
         compiler_params=pltpu.CompilerParams(vmem_limit_bytes=COMPARE_VMEM),
+        cost_estimate=pl.CostEstimate(
+            flops=12 * columns * depth * ranges // 2, bytes_accessed=40 * 2**20, transcendentals=0
+        ),
         name="compare",
-    )(count, h, pings, pings, own, inverse, power)
+    )(count, h, pings, pings, own, inverse, power, begun, edge)
 
 
 def body(raw_pings, focus_matrix, start_angle, ping_count):
@@ -284,10 +382,14 @@
     plain = jnp.concatenate([focus_matrix[0], focus_matrix[1]], axis=1)
     counts = ping_count[jnp.stack([position, neighbour])]
     received, plain, turned, counts = lax.optimization_barrier((received, plain, turned, counts))
-    own_pings = received.reshape(received.shape[0], -1)
-    other_pings = shifted(own_pings, "sector", -1)
+    width = raw_pings.shape[3] // PIECES
+    own_pings = [
+        received[:, :, piece * width:(piece + 1) * width].reshape(received.shape[0], -1) for piece in range(PIECES)
+    ]
+    other_pings = [shifted(piece, "sector", -1) for piece in own_pings]
     own, inverse, power = focus(counts[:1], plain, own_pings)
-    coherence, interferogram = compare(counts[1:], turned, other_pings, own, inverse, power)
+    begun, edge = compare_first(counts[1:], turned, other_pings[0], own, inverse)
+    coherence, interferogram = compare(counts[1:], turned, other_pings[1], own, inverse, power, begun, edge)
     return (coherence[None], interferogram[None])
 
 

time: 117 us -> 115 us (0.983)
  waiting for transfers between devices: 32.9 us -> 28.7 us
  Pallas kernels: 50.1 us -> 52.7 us
    ppermute x1 -> x2, waiting for transfers between devices: 4.25 us -> 0.01 us  [shifted(): return lax.ppermute(block, axis, route)]
    unnamed x13 -> x16, local copies, waits for them, and re-layouts: 3.45 us -> 1.37 us
    pallas_call x1 -> x2, Pallas kernels: 33.3 us -> 35.2 us  [the longest x1 21.6 us: compare(): pl.pallas_call(functools.partial(compare_kernel, first=first, chunks=chun...]
    slice x0 -> x1, local copies, waits for them, and re-layouts: none -> 1.47 us  [body(): received[:, :, piece * width:(piece + 1) * width]]
    ppermute x1 -> x2, starting transfers between devices: 9.89 us -> 10.2 us  [shifted(): return lax.ppermute(block, axis, route)]
  transfers between devices with their start and end apart: 2 -> 3, of which waited for: 2 -> 1; matrix products, arithmetic and copies ran while one was open for 9% -> 10% of each run, Pallas kernels for 14% -> 27%
where the time goes in v4:
time: 115 us
  Pallas kernels  52.7 us (46%)
  waiting for transfers between devices  28.7 us (25%)
  starting transfers between devices  17.8 us (15%)
  other arithmetic  8.56 us (7%)
  local copies, waits for them, and re-layouts  5.01 us (4%)
  between operations  2.17 us (2%)
    all_to_all x1, waiting for transfers between devices, body(): lax.all_to_all(raw_pings, 'sector', split_axis=0, concat_axis=1, tiled=True)  28.7 us
    pallas_call x1, Pallas kernels, compare(): pl.pallas_call(functools.partial(compare_kernel, first=first, chunks=chun...  21.6 us
    pallas_call x1, Pallas kernels, focus(): pl.pallas_call(functools.partial(focus_kernel, chunks=chunks, rows=rows),...  17.4 us
    pallas_call x1, Pallas kernels, compare_first(): pl.pallas_call(functools.partial(first_kernel, rows=rows), grid=(chunks,)...  13.7 us
    ppermute x2, starting transfers between devices, shifted(): return lax.ppermute(block, axis, route)  10.2 us
    all_to_all x1, starting transfers between devices, body(): lax.all_to_all(raw_pings, 'sector', split_axis=0, concat_axis=1, tiled=True)  7.56 us
    convert_element_type x1, other arithmetic, body(): part.astype(jnp.bfloat16)  2.97 us
    concatenate x1, other arithmetic, body(): jnp.concatenate([part.astype(jnp.bfloat16) for part in turned], axis=1)  2.76 us
  transfers between devices with their start and end apart: 3, of which 1 were waited for; matrix products, arithmetic and copies ran while one was open for 10% of the time, Pallas kernels for 27%

profile of v4, /device:TPU:0, one launch (start us, length us, event | category | flops | bytes accessed | tf_op | source)
XLA Modules:
  0.0 114.9 jit_solution(2111487285125398765)
XLA Ops:
  0.6 0.0 copy-start
  0.7 7.6 %all-to-all-start = ((bf16[16,32,2,1024]{3,2,1,0:T(2,128)(2,1)}), bf16[16,32,2,1024]{3,2,1,0:T(2,128)(2,1)S(1)}, u32[]{:S(2)}, u32[]{:S(2)}) async-start(bf16[16,32,2,1024]{3,2,1,0:T(2,128)(2,1)} %param.4), calls=%async_computation | async-start | bytes 4194304 | tf_op jit(solution)/shard_map/all_to_all | solution.py:374
  8.2 0.7 fusion.15
  10.2 0.1 fusion.12
  10.3 0.6 gather_fusion
  10.9 0.1 fusion.10
  11.0 3.0 %fusion.1 = (bf16[2048,512]{1,0:T(8,128)(2,1)S(1)}, bf16[2048,512]{1,0:T(8,128)(2,1)S(1)}) fusion(f32[2048]{0:T(1024)S(1)} %get-tuple-element.34, f32[2048]{0:T(1024)S(1)} %get-tuple-element.35, bf16[2,2048,512]{2,1,0:T(8,128)(2,1)} %param.5), kind=kLoop, calls=%fused_computation.6 | loop fusion | flops 10485760 | bytes 8404992 | tf_op jit(solution)/shard_map/convert_element_type | solution.py:381
  13.9 0.0 copy-start.5
  14.0 2.8 %pad_maximum_fusion.1.h_ref = bf16[2048,1024]{1,0:T(8,128)(2,1)} fusion(bf16[2048,512]{1,0:T(8,128)(2,1)S(1)} %get-tuple-element.25, bf16[2048,512]{1,0:T(8,128)(2,1)S(1)} %get-tuple-element.24), kind=kLoop, calls=%fused_computation.10 | loop fusion | flops 8388608 | bytes 8388608 | tf_op jit(solution)/shard_map/concatenate | solution.py:381
  16.7 0.9 copy-done.5
  17.6 0.3 slice_bitcast_fusion.1
  17.9 2.7 %pad_maximum_fusion.h_ref = bf16[2048,1024]{1,0:T(8,128)(2,1)} fusion(bf16[2048,512]{1,0:T(8,128)(2,1)S(1)} %get-tuple-element.27, bf16[2048,512]{1,0:T(8,128)(2,1)S(1)} %get-tuple-element.26), kind=kLoop, calls=%fused_computation.9 | loop fusion | flops 8388608 | bytes 8388608 | tf_op jit(solution)/shard_map/concatenate | solution.py:382
  20.5 28.7 %all-to-all-done = bf16[16,32,2,1024]{3,2,1,0:T(2,128)(2,1)S(1)} async-done(((bf16[16,32,2,1024]{3,2,1,0:T(2,128)(2,1)}), bf16[16,32,2,1024]{3,2,1,0:T(2,128)(2,1)S(1)}, u32[]{:S(2)}, u32[]{:S(2)}) %all-to-all-start) | async-done | bytes 2097184 | tf_op jit(solution)/shard_map/all_to_all | solution.py:374
  49.2 1.5 %fusion.13 = (bf16[512,2,512]{2,1,0:T(2,128)(2,1)S(1)}, bf16[512,2,512]{2,1,0:T(2,128)(2,1)S(1)}) fusion(bf16[512,2,1024]{2,1,0:T(2,128)(2,1)S(1)} %bitcast.30), kind=kLoop, calls=%fused_computation.27 | loop fusion | bytes 4194304 | tf_op jit(solution)/shard_map/slice | solution.py:387
  50.7 0.2 copy.7
  50.9 9.9 %collective-permute-start.1 = (bf16[512,1024]{1,0:T(8,128)(2,1)S(1)}, bf16[512,1024]{1,0:T(8,128)(2,1)S(1)}, u32[]{:S(2)}, u32[]{:S(2)}) collective-permute-start(bf16[512,1024]{1,0:T(8,128)(2,1)S(1)} %bitcast.27), channel_id=1, source_target_pairs={{1,0},{2,1},{3,2},{4,3},{5,4},{6,5},{7,6},{8,7},{9,8},{10,9},{11,1... | collective-permute-start | bytes 3145736 | tf_op jit(solution)/shard_map/ppermute | solution.py:23
  60.8 0.2 copy.6
  61.1 0.3 collective-permute-start
  61.4 0.6 fusion.14
  62.0 17.4 %focus.1 = (f32[2,2048,1024]{2,1,0:T(8,128)}, f32[8,1024]{1,0:T(8,128)S(1)}, bf16[2048,1024]{1,0:T(8,128)(2,1)S(1)}) custom-call(s32[1]{0:T(128)} %get-tuple-element.30.count_ref, bf16[2048,1024]{1,0:T(8,128)(2,1)S(1)} %copy-done.3, bf16[512,1024]{1,0:T(8,128)(2,1)S(1)} %bitcast.28, bf16[512,1024]{1,0:T(8,128)(2,1)S(1)} %bitcast.29, ...), custom_call_target="tpu_custom_call" | custom-call | flops 8589934592 | bytes 33554432 | tf_op jit(solution)/shard_map/focus/pallas_call | solution.py:170
  79.4 0.0 collective-permute-done.1.xr_ref.xi_ref
  79.4 13.7 %compare_first.1 = (bf16[3,2048,512]{2,1,0:T(8,128)(2,1)}, bf16[2048,384]{1,0:T(8,128)(2,1)S(1)}) custom-call(s32[1]{0:T(128)} %get-tuple-element.31.count_ref, bf16[2048,1024]{1,0:T(8,128)(2,1)S(1)} %copy-done.2, bf16[512,1024]{1,0:T(8,128)(2,1)S(1)} %collective-permute-done.1.xr_ref.xi_ref, bf16[512,1024]{1,0:T(8,128)(2,1)S(1)} %collective-permute-done.1.xr_ref.xi_ref, ...), custom_call_target="tpu_custom_call" | custom-call | flops 4294967296 | bytes 25165824 | tf_op jit(solution)/shard_map/compare_first/pallas_call | solution.py:247
  93.1 0.0 collective-permute-done.xr_ref.xi_ref
  93.1 21.6 %compare.8 = (f32[2048,1024]{1,0:T(8,128)}, bf16[2,2048,1024]{2,1,0:T(8,128)(2,1)}) custom-call(s32[1]{0:T(128)} %get-tuple-element.31.count_ref, bf16[2048,1024]{1,0:T(8,128)(2,1)S(1)} %copy-done.2, bf16[512,1024]{1,0:T(8,128)(2,1)S(1)} %collective-permute-done.xr_ref.xi_ref, bf16[512,1024]{1,0:T(8,128)(2,1)S(1)} %collective-permute-done.xr_ref.xi_ref, ...), custom_call_target="tpu_custom_call" | custom-call | flops 6442450944 | bytes 41943040 | tf_op jit(solution)/shard_map/compare/pallas_call | solution.py:338
  (12 shorter events, 0.0 us)
Async XLA Ops:
  0.6 9.6 %copy-start = (s32[16]{0:T(128)S(1)}, s32[16]{0:T(128)}, u32[]{:S(2)}) copy-start(s32[16]{0:T(128)} %param.7) | copy-start | bytes 196
  0.6 7.6 %copy-start.6 = (s32[16]{0:T(128)S(1)}, s32[16]{0:T(128)}, u32[]{:S(2)}) copy-start(s32[16]{0:T(128)} %param.6) | copy-start | bytes 196
  0.7 48.5 %all-to-all-start = ((bf16[16,32,2,1024]{3,2,1,0:T(2,128)(2,1)}), bf16[16,32,2,1024]{3,2,1,0:T(2,128)(2,1)S(1)}, u32[]{:S(2)}, u32[]{:S(2)}) async-start(bf16[16,32,2,1024]{3,2,1,0:T(2,128)(2,1)} %param.4), calls=%async_computation | async-start | bytes 4194304 | tf_op jit(solution)/shard_map/all_to_all | solution.py:374
  13.9 3.6 %copy-start.5 = (bf16[2,2048,512]{2,1,0:T(8,128)(2,1)S(1)}, bf16[2,2048,512]{2,1,0:T(8,128)(2,1)}, u32[]{:S(2)}) copy-start(bf16[2,2048,512]{2,1,0:T(8,128)(2,1)} %param.5) | copy-start | bytes 12582916
  49.2 12.8 %copy-start.3 = (bf16[2048,1024]{1,0:T(8,128)(2,1)S(1)}, bf16[2048,1024]{1,0:T(8,128)(2,1)}, u32[]{:S(2)}) copy-start(bf16[2048,1024]{1,0:T(8,128)(2,1)} %pad_maximum_fusion.h_ref) | copy-start | bytes 12582916
  50.9 28.5 %collective-permute-start.1 = (bf16[512,1024]{1,0:T(8,128)(2,1)S(1)}, bf16[512,1024]{1,0:T(8,128)(2,1)S(1)}, u32[]{:S(2)}, u32[]{:S(2)}) collective-permute-start(bf16[512,1024]{1,0:T(8,128)(2,1)S(1)} %bitcast.27), channel_id=1, source_target_pairs={{1,0},{2,1},{3,2},{4,3},{5,4},{6,5},{7,6},{8,7},{9,8},{10,9},{11,1... | collective-permute-start | bytes 3145736 | tf_op jit(solution)/shard_map/ppermute | solution.py:23
  61.1 32.1 %collective-permute-start = (bf16[512,1024]{1,0:T(8,128)(2,1)S(1)}, bf16[512,1024]{1,0:T(8,128)(2,1)S(1)}, u32[]{:S(2)}, u32[]{:S(2)}) collective-permute-start(bf16[512,1024]{1,0:T(8,128)(2,1)S(1)} %bitcast.24), channel_id=1, source_target_pairs={{1,0},{2,1},{3,2},{4,3},{5,4},{6,5},{7,6},{8,7},{9,8},{10,9},{11,1... | collective-permute-start | bytes 3145736 | tf_op jit(solution)/shard_map/ppermute | solution.py:23
  62.0 17.4 %copy-start.2 = (bf16[2048,1024]{1,0:T(8,128)(2,1)S(1)}, bf16[2048,1024]{1,0:T(8,128)(2,1)}, u32[]{:S(2)}) copy-start(bf16[2048,1024]{1,0:T(8,128)(2,1)} %pad_maximum_fusion.1.h_ref) | copy-start | bytes 12582916
  79.4 13.7 %copy-start.4 = (bf16[2048,1024]{1,0:T(8,128)(2,1)}, bf16[2048,1024]{1,0:T(8,128)(2,1)S(1)}, u32[]{:S(2)}) copy-start(bf16[2048,1024]{1,0:T(8,128)(2,1)S(1)} %get-tuple-element.19.power_ref) | copy-start | bytes 12582916
  93.1 21.6 %copy-start.1 = (s32[16]{0:T(128)S(1)}, s32[16]{0:T(128)}, u32[]{:S(2)}) copy-start(s32[16]{0:T(128)} %param.7) | copy-start | bytes 196

commit v5 on v4

--- a/solution.py
+++ b/solution.py
@@ -380,16 +380,19 @@
     turned = [h_real * cosine - h_imag * sine, h_real * sine + h_imag * cosine]
     turned = jnp.concatenate([part.astype(jnp.bfloat16) for part in turned], axis=1)
     plain = jnp.concatenate([focus_matrix[0], focus_matrix[1]], axis=1)
-    counts = ping_count[jnp.stack([position, neighbour])]
-    received, plain, turned, counts = lax.optimization_barrier((received, plain, turned, counts))
+    own_count = lax.dynamic_slice_in_dim(ping_count, position, 1)
+    other_count = lax.dynamic_slice_in_dim(ping_count, neighbour, 1)
+    received, plain, turned, own_count, other_count = lax.optimization_barrier(
+        (received, plain, turned, own_count, other_count)
+    )
     width = raw_pings.shape[3] // PIECES
     own_pings = [
         received[:, :, piece * width:(piece + 1) * width].reshape(received.shape[0], -1) for piece in range(PIECES)
     ]
     other_pings = [shifted(piece, "sector", -1) for piece in own_pings]
-    own, inverse, power = focus(counts[:1], plain, own_pings)
-    begun, edge = compare_first(counts[1:], turned, other_pings[0], own, inverse)
-    coherence, interferogram = compare(counts[1:], turned, other_pings[1], own, inverse, power, begun, edge)
+    own, inverse, power = focus(own_count, plain, own_pings)
+    begun, edge = compare_first(other_count, turned, other_pings[0], own, inverse)
+    coherence, interferogram = compare(other_count, turned, other_pings[1], own, inverse, power, begun, edge)
     return (coherence[None], interferogram[None])
 
 

time: 115 us -> 114 us (level)
  transfers between devices with their start and end apart: 3 -> 3, of which waited for: 1 -> 1; matrix products, arithmetic and copies ran while one was open for 10% -> 9% of each run, Pallas kernels for 27% -> 27%
where the time goes in v5:
time: 114 us
  Pallas kernels  52 us (46%)
  waiting for transfers between devices  28.8 us (25%)
  starting transfers between devices  17.8 us (16%)
  other arithmetic  8.47 us (7%)
  local copies, waits for them, and re-layouts  4.31 us (4%)
  between operations  2.21 us (2%)
    all_to_all x1, waiting for transfers between devices, body(): lax.all_to_all(raw_pings, 'sector', split_axis=0, concat_axis=1, tiled=True)  28.8 us
    pallas_call x1, Pallas kernels, compare(): pl.pallas_call(functools.partial(compare_kernel, first=first, chunks=chun...  21.2 us
    pallas_call x1, Pallas kernels, focus(): pl.pallas_call(functools.partial(focus_kernel, chunks=chunks, rows=rows),...  17.2 us
    pallas_call x1, Pallas kernels, compare_first(): pl.pallas_call(functools.partial(first_kernel, rows=rows), grid=(chunks,)...  13.6 us
    ppermute x2, starting transfers between devices, shifted(): return lax.ppermute(block, axis, route)  10.2 us
    all_to_all x1, starting transfers between devices, body(): lax.all_to_all(raw_pings, 'sector', split_axis=0, concat_axis=1, tiled=True)  7.56 us
    convert_element_type x1, other arithmetic, body(): part.astype(jnp.bfloat16)  2.97 us
    concatenate x1, other arithmetic, body(): jnp.concatenate([part.astype(jnp.bfloat16) for part in turned], axis=1)  2.76 us
  transfers between devices with their start and end apart: 3, of which 1 were waited for; matrix products, arithmetic and copies ran while one was open for 9% of the time, Pallas kernels for 27%

profile of v5, /device:TPU:0, one launch (start us, length us, event | category | flops | bytes accessed | tf_op | source)
XLA Modules:
  0.0 113.6 jit_solution(10781504409799901399)
XLA Ops:
  0.6 7.6 %all-to-all-start = ((bf16[16,32,2,1024]{3,2,1,0:T(2,128)(2,1)}), bf16[16,32,2,1024]{3,2,1,0:T(2,128)(2,1)S(1)}, u32[]{:S(2)}, u32[]{:S(2)}) async-start(bf16[16,32,2,1024]{3,2,1,0:T(2,128)(2,1)} %param.4), calls=%async_computation | async-start | bytes 4194304 | tf_op jit(solution)/shard_map/all_to_all | solution.py:374
  8.2 0.6 fusion.14
  10.1 0.6 fusion.13
  10.8 0.1 fusion.10
  10.8 3.0 %fusion.1 = (bf16[2048,512]{1,0:T(8,128)(2,1)S(1)}, bf16[2048,512]{1,0:T(8,128)(2,1)S(1)}) fusion(f32[2048]{0:T(1024)S(1)} %get-tuple-element.36, f32[2048]{0:T(1024)S(1)} %get-tuple-element.37, bf16[2,2048,512]{2,1,0:T(8,128)(2,1)} %param.5), kind=kLoop, calls=%fused_computation.5 | loop fusion | flops 10485760 | bytes 8404992 | tf_op jit(solution)/shard_map/convert_element_type | solution.py:381
  13.8 0.0 copy-start.3
  13.8 2.8 %pad_maximum_fusion.1.h_ref = bf16[2048,1024]{1,0:T(8,128)(2,1)} fusion(bf16[2048,512]{1,0:T(8,128)(2,1)S(1)} %get-tuple-element.27, bf16[2048,512]{1,0:T(8,128)(2,1)S(1)} %get-tuple-element.26), kind=kLoop, calls=%fused_computation.9 | loop fusion | flops 8388608 | bytes 8388608 | tf_op jit(solution)/shard_map/concatenate | solution.py:381
  16.6 0.9 copy-done.3
  17.4 0.3 slice_bitcast_fusion.1
  17.7 2.7 %pad_maximum_fusion.h_ref = bf16[2048,1024]{1,0:T(8,128)(2,1)} fusion(bf16[2048,512]{1,0:T(8,128)(2,1)S(1)} %get-tuple-element.29, bf16[2048,512]{1,0:T(8,128)(2,1)S(1)} %get-tuple-element.28), kind=kLoop, calls=%fused_computation.8 | loop fusion | flops 8388608 | bytes 8388608 | tf_op jit(solution)/shard_map/concatenate | solution.py:382
  20.4 28.8 %all-to-all-done = bf16[16,32,2,1024]{3,2,1,0:T(2,128)(2,1)S(1)} async-done(((bf16[16,32,2,1024]{3,2,1,0:T(2,128)(2,1)}), bf16[16,32,2,1024]{3,2,1,0:T(2,128)(2,1)S(1)}, u32[]{:S(2)}, u32[]{:S(2)}) %all-to-all-start) | async-done | bytes 2097184 | tf_op jit(solution)/shard_map/all_to_all | solution.py:374
  49.2 1.5 %fusion.12 = (bf16[512,2,512]{2,1,0:T(2,128)(2,1)S(1)}, bf16[512,2,512]{2,1,0:T(2,128)(2,1)S(1)}) fusion(bf16[512,2,1024]{2,1,0:T(2,128)(2,1)S(1)} %bitcast.26), kind=kLoop, calls=%fused_computation.23 | loop fusion | bytes 4194304 | tf_op jit(solution)/shard_map/slice | solution.py:390
  50.7 0.2 copy.7
  50.9 9.9 %collective-permute-start.1 = (bf16[512,1024]{1,0:T(8,128)(2,1)S(1)}, bf16[512,1024]{1,0:T(8,128)(2,1)S(1)}, u32[]{:S(2)}, u32[]{:S(2)}) collective-permute-start(bf16[512,1024]{1,0:T(8,128)(2,1)S(1)} %bitcast.23), channel_id=1, source_target_pairs={{1,0},{2,1},{3,2},{4,3},{5,4},{6,5},{7,6},{8,7},{9,8},{10,9},{11,1... | collective-permute-start | bytes 3145736 | tf_op jit(solution)/shard_map/ppermute | solution.py:23
  60.8 0.2 copy.6
  61.0 0.0 copy-start
  61.1 0.3 collective-permute-start
  61.4 17.2 %focus.1 = (f32[2,2048,1024]{2,1,0:T(8,128)}, f32[8,1024]{1,0:T(8,128)S(1)}, bf16[2048,1024]{1,0:T(8,128)(2,1)S(1)}) custom-call(s32[1]{0:T(128)} %get-tuple-element.17.count_ref, bf16[2048,1024]{1,0:T(8,128)(2,1)S(1)} %copy-done.1, bf16[512,1024]{1,0:T(8,128)(2,1)S(1)} %bitcast.24, bf16[512,1024]{1,0:T(8,128)(2,1)S(1)} %bitcast.25, ...), custom_call_target="tpu_custom_call" | custom-call | flops 8589934592 | bytes 33554432 | tf_op jit(solution)/shard_map/focus/pallas_call | solution.py:170
  78.6 0.0 collective-permute-done.1.xr_ref.xi_ref
  78.6 0.0 copy-done
  78.6 13.6 %compare_first.1 = (bf16[3,2048,512]{2,1,0:T(8,128)(2,1)}, bf16[2048,384]{1,0:T(8,128)(2,1)S(1)}) custom-call(s32[1]{0:T(128)} %get-tuple-element.14.count_ref, bf16[2048,1024]{1,0:T(8,128)(2,1)S(1)} %copy-done, bf16[512,1024]{1,0:T(8,128)(2,1)S(1)} %collective-permute-done.1.xr_ref.xi_ref, bf16[512,1024]{1,0:T(8,128)(2,1)S(1)} %collective-permute-done.1.xr_ref.xi_ref, ...), custom_call_target="tpu_custom_call" | custom-call | flops 4294967296 | bytes 25165824 | tf_op jit(solution)/shard_map/compare_first/pallas_call | solution.py:247
  92.2 0.0 copy-done.2
  92.2 0.0 collective-permute-done.xr_ref.xi_ref
  92.2 21.2 %compare.8 = (f32[2048,1024]{1,0:T(8,128)}, bf16[2,2048,1024]{2,1,0:T(8,128)(2,1)}) custom-call(s32[1]{0:T(128)} %get-tuple-element.14.count_ref, bf16[2048,1024]{1,0:T(8,128)(2,1)S(1)} %copy-done, bf16[512,1024]{1,0:T(8,128)(2,1)S(1)} %collective-permute-done.xr_ref.xi_ref, bf16[512,1024]{1,0:T(8,128)(2,1)S(1)} %collective-permute-done.xr_ref.xi_ref, ...), custom_call_target="tpu_custom_call" | custom-call | flops 6442450944 | bytes 41943040 | tf_op jit(solution)/shard_map/compare/pallas_call | solution.py:338
  (7 shorter events, 0.0 us)
Async XLA Ops:
  0.6 7.6 %copy-start.4 = (s32[16]{0:T(128)S(1)}, s32[16]{0:T(128)}, u32[]{:S(2)}) copy-start(s32[16]{0:T(128)} %param.6) | copy-start | bytes 196
  0.6 9.5 %copy-start.5 = (s32[16]{0:T(128)S(1)}, s32[16]{0:T(128)}, u32[]{:S(2)}) copy-start(s32[16]{0:T(128)} %param.7) | copy-start | bytes 196
  0.6 48.5 %all-to-all-start = ((bf16[16,32,2,1024]{3,2,1,0:T(2,128)(2,1)}), bf16[16,32,2,1024]{3,2,1,0:T(2,128)(2,1)S(1)}, u32[]{:S(2)}, u32[]{:S(2)}) async-start(bf16[16,32,2,1024]{3,2,1,0:T(2,128)(2,1)} %param.4), calls=%async_computation | async-start | bytes 4194304 | tf_op jit(solution)/shard_map/all_to_all | solution.py:374
  13.8 3.6 %copy-start.3 = (bf16[2,2048,512]{2,1,0:T(8,128)(2,1)S(1)}, bf16[2,2048,512]{2,1,0:T(8,128)(2,1)}, u32[]{:S(2)}) copy-start(bf16[2,2048,512]{2,1,0:T(8,128)(2,1)} %param.5) | copy-start | bytes 12582916
  49.2 12.2 %copy-start.1 = (bf16[2048,1024]{1,0:T(8,128)(2,1)S(1)}, bf16[2048,1024]{1,0:T(8,128)(2,1)}, u32[]{:S(2)}) copy-start(bf16[2048,1024]{1,0:T(8,128)(2,1)} %pad_maximum_fusion.h_ref) | copy-start | bytes 12582916
  50.9 27.7 %collective-permute-start.1 = (bf16[512,1024]{1,0:T(8,128)(2,1)S(1)}, bf16[512,1024]{1,0:T(8,128)(2,1)S(1)}, u32[]{:S(2)}, u32[]{:S(2)}) collective-permute-start(bf16[512,1024]{1,0:T(8,128)(2,1)S(1)} %bitcast.23), channel_id=1, source_target_pairs={{1,0},{2,1},{3,2},{4,3},{5,4},{6,5},{7,6},{8,7},{9,8},{10,9},{11,1... | collective-permute-start | bytes 3145736 | tf_op jit(solution)/shard_map/ppermute | solution.py:23
  61.0 17.6 %copy-start = (bf16[2048,1024]{1,0:T(8,128)(2,1)S(1)}, bf16[2048,1024]{1,0:T(8,128)(2,1)}, u32[]{:S(2)}) copy-start(bf16[2048,1024]{1,0:T(8,128)(2,1)} %pad_maximum_fusion.1.h_ref) | copy-start | bytes 12582916
  61.1 31.1 %collective-permute-start = (bf16[512,1024]{1,0:T(8,128)(2,1)S(1)}, bf16[512,1024]{1,0:T(8,128)(2,1)S(1)}, u32[]{:S(2)}, u32[]{:S(2)}) collective-permute-start(bf16[512,1024]{1,0:T(8,128)(2,1)S(1)} %bitcast.20), channel_id=1, source_target_pairs={{1,0},{2,1},{3,2},{4,3},{5,4},{6,5},{7,6},{8,7},{9,8},{10,9},{11,1... | collective-permute-start | bytes 3145736 | tf_op jit(solution)/shard_map/ppermute | solution.py:23
  78.6 13.6 %copy-start.2 = (bf16[2048,1024]{1,0:T(8,128)(2,1)}, bf16[2048,1024]{1,0:T(8,128)(2,1)S(1)}, u32[]{:S(2)}) copy-start(bf16[2048,1024]{1,0:T(8,128)(2,1)S(1)} %get-tuple-element.21.power_ref) | copy-start | bytes 12582916

commit v6 on v5

--- a/solution.py
+++ b/solution.py
@@ -386,9 +386,11 @@
         (received, plain, turned, own_count, other_count)
     )
     width = raw_pings.shape[3] // PIECES
-    own_pings = [
-        received[:, :, piece * width:(piece + 1) * width].reshape(received.shape[0], -1) for piece in range(PIECES)
-    ]
+    own_pings = []
+    for piece in range(PIECES):
+        part = received[:, :, piece * width:(piece + 1) * width].reshape(received.shape[0], -1)
+        part, received = lax.optimization_barrier((part, received))
+        own_pings.append(part)
     other_pings = [shifted(piece, "sector", -1) for piece in own_pings]
     own, inverse, power = focus(own_count, plain, own_pings)
     begun, edge = compare_first(other_count, turned, other_pings[0], own, inverse)

time: 114 us -> 114 us (level)
  transfers between devices with their start and end apart: 3 -> 3, of which waited for: 1 -> 1; matrix products, arithmetic and copies ran while one was open for 9% -> 10% of each run, Pallas kernels for 27% -> 27%
where the time goes in v6:
time: 114 us
  Pallas kernels  52.1 us (46%)
  waiting for transfers between devices  28.8 us (25%)
  starting transfers between devices  17.8 us (16%)
  other arithmetic  8.47 us (7%)
  local copies, waits for them, and re-layouts  4.33 us (4%)
  between operations  2.21 us (2%)
    all_to_all x1, waiting for transfers between devices, body(): lax.all_to_all(raw_pings, 'sector', split_axis=0, concat_axis=1, tiled=True)  28.8 us
    pallas_call x1, Pallas kernels, compare(): pl.pallas_call(functools.partial(compare_kernel, first=first, chunks=chun...  21.2 us
    pallas_call x1, Pallas kernels, focus(): pl.pallas_call(functools.partial(focus_kernel, chunks=chunks, rows=rows),...  17.4 us
    pallas_call x1, Pallas kernels, compare_first(): pl.pallas_call(functools.partial(first_kernel, rows=rows), grid=(chunks,)...  13.6 us
    ppermute x2, starting transfers between devices, shifted(): return lax.ppermute(block, axis, route)  10.2 us
    all_to_all x1, starting transfers between devices, body(): lax.all_to_all(raw_pings, 'sector', split_axis=0, concat_axis=1, tiled=True)  7.56 us
    convert_element_type x1, other arithmetic, body(): part.astype(jnp.bfloat16)  2.97 us
    concatenate x1, other arithmetic, body(): jnp.concatenate([part.astype(jnp.bfloat16) for part in turned], axis=1)  2.76 us
  transfers between devices with their start and end apart: 3, of which 1 were waited for; matrix products, arithmetic and copies ran while one was open for 10% of the time, Pallas kernels for 27%

profile of v6, /device:TPU:0, one launch (start us, length us, event | category | flops | bytes accessed | tf_op | source)
XLA Modules:
  0.0 113.7 jit_solution(14658208139625849668)
XLA Ops:
  0.6 7.6 %all-to-all-start = ((bf16[16,32,2,1024]{3,2,1,0:T(2,128)(2,1)}), bf16[16,32,2,1024]{3,2,1,0:T(2,128)(2,1)S(1)}, u32[]{:S(2)}, u32[]{:S(2)}) async-start(bf16[16,32,2,1024]{3,2,1,0:T(2,128)(2,1)} %param.4), calls=%async_computation | async-start | bytes 4194304 | tf_op jit(solution)/shard_map/all_to_all | solution.py:374
  8.2 0.6 fusion.13
  10.1 0.7 fusion.12
  10.8 0.1 fusion.10
  10.9 3.0 %fusion.1 = (bf16[2048,512]{1,0:T(8,128)(2,1)S(1)}, bf16[2048,512]{1,0:T(8,128)(2,1)S(1)}) fusion(f32[2048]{0:T(1024)S(1)} %get-tuple-element.40, f32[2048]{0:T(1024)S(1)} %get-tuple-element.41, bf16[2,2048,512]{2,1,0:T(8,128)(2,1)} %param.5), kind=kLoop, calls=%fused_computation.5 | loop fusion | flops 10485760 | bytes 8404992 | tf_op jit(solution)/shard_map/convert_element_type | solution.py:381
  13.8 0.0 copy-start.3
  13.9 2.8 %pad_maximum_fusion.1.h_ref = bf16[2048,1024]{1,0:T(8,128)(2,1)} fusion(bf16[2048,512]{1,0:T(8,128)(2,1)S(1)} %get-tuple-element.33, bf16[2048,512]{1,0:T(8,128)(2,1)S(1)} %get-tuple-element.32), kind=kLoop, calls=%fused_computation.9 | loop fusion | flops 8388608 | bytes 8388608 | tf_op jit(solution)/shard_map/concatenate | solution.py:381
  16.6 0.9 copy-done.3
  17.5 0.3 slice_bitcast_fusion.1
  17.8 2.7 %pad_maximum_fusion.h_ref = bf16[2048,1024]{1,0:T(8,128)(2,1)} fusion(bf16[2048,512]{1,0:T(8,128)(2,1)S(1)} %get-tuple-element.35, bf16[2048,512]{1,0:T(8,128)(2,1)S(1)} %get-tuple-element.34), kind=kLoop, calls=%fused_computation.8 | loop fusion | flops 8388608 | bytes 8388608 | tf_op jit(solution)/shard_map/concatenate | solution.py:382
  20.4 28.8 %all-to-all-done = bf16[16,32,2,1024]{3,2,1,0:T(2,128)(2,1)S(1)} async-done(((bf16[16,32,2,1024]{3,2,1,0:T(2,128)(2,1)}), bf16[16,32,2,1024]{3,2,1,0:T(2,128)(2,1)S(1)}, u32[]{:S(2)}, u32[]{:S(2)}) %all-to-all-start) | async-done | bytes 2097184 | tf_op jit(solution)/shard_map/all_to_all | solution.py:374
  49.2 0.7 slice.16
  49.9 0.2 copy.6
  50.2 9.9 %collective-permute-start.1 = (bf16[512,1024]{1,0:T(8,128)(2,1)S(1)}, bf16[512,1024]{1,0:T(8,128)(2,1)S(1)}, u32[]{:S(2)}, u32[]{:S(2)}) collective-permute-start(bf16[512,1024]{1,0:T(8,128)(2,1)S(1)} %bitcast.20), channel_id=1, source_target_pairs={{1,0},{2,1},{3,2},{4,3},{5,4},{6,5},{7,6},{8,7},{9,8},{10,9},{11,1... | collective-permute-start | bytes 3145736 | tf_op jit(solution)/shard_map/ppermute | solution.py:23
  60.1 0.7 slice.17
  60.8 0.2 copy.7
  61.0 0.0 copy-start
  61.0 0.3 collective-permute-start
  61.4 17.4 %focus.1 = (f32[2,2048,1024]{2,1,0:T(8,128)}, f32[8,1024]{1,0:T(8,128)S(1)}, bf16[2048,1024]{1,0:T(8,128)(2,1)S(1)}) custom-call(s32[1]{0:T(128)} %get-tuple-element.22.count_ref, bf16[2048,1024]{1,0:T(8,128)(2,1)S(1)} %copy-done.1, bf16[512,1024]{1,0:T(8,128)(2,1)S(1)} %bitcast.21, bf16[512,1024]{1,0:T(8,128)(2,1)S(1)} %bitcast.22, ...), custom_call_target="tpu_custom_call" | custom-call | flops 8589934592 | bytes 33554432 | tf_op jit(solution)/shard_map/focus/pallas_call | solution.py:170
  78.8 0.0 collective-permute-done.1.xr_ref.xi_ref
  78.8 0.0 copy-done
  78.8 13.6 %compare_first.1 = (bf16[3,2048,512]{2,1,0:T(8,128)(2,1)}, bf16[2048,384]{1,0:T(8,128)(2,1)S(1)}) custom-call(s32[1]{0:T(128)} %get-tuple-element.17.count_ref, bf16[2048,1024]{1,0:T(8,128)(2,1)S(1)} %copy-done, bf16[512,1024]{1,0:T(8,128)(2,1)S(1)} %collective-permute-done.1.xr_ref.xi_ref, bf16[512,1024]{1,0:T(8,128)(2,1)S(1)} %collective-permute-done.1.xr_ref.xi_ref, ...), custom_call_target="tpu_custom_call" | custom-call | flops 4294967296 | bytes 25165824 | tf_op jit(solution)/shard_map/compare_first/pallas_call | solution.py:247
  92.3 0.0 collective-permute-done.xr_ref.xi_ref
  92.3 21.2 %compare.8 = (f32[2048,1024]{1,0:T(8,128)}, bf16[2,2048,1024]{2,1,0:T(8,128)(2,1)}) custom-call(s32[1]{0:T(128)} %get-tuple-element.17.count_ref, bf16[2048,1024]{1,0:T(8,128)(2,1)S(1)} %copy-done, bf16[512,1024]{1,0:T(8,128)(2,1)S(1)} %collective-permute-done.xr_ref.xi_ref, bf16[512,1024]{1,0:T(8,128)(2,1)S(1)} %collective-permute-done.xr_ref.xi_ref, ...), custom_call_target="tpu_custom_call" | custom-call | flops 6442450944 | bytes 41943040 | tf_op jit(solution)/shard_map/compare/pallas_call | solution.py:338
  (8 shorter events, 0.0 us)
Async XLA Ops:
  0.6 7.6 %copy-start.4 = (s32[16]{0:T(128)S(1)}, s32[16]{0:T(128)}, u32[]{:S(2)}) copy-start(s32[16]{0:T(128)} %param.6) | copy-start | bytes 196
  0.6 9.5 %copy-start.5 = (s32[16]{0:T(128)S(1)}, s32[16]{0:T(128)}, u32[]{:S(2)}) copy-start(s32[16]{0:T(128)} %param.7) | copy-start | bytes 196
  0.6 48.5 %all-to-all-start = ((bf16[16,32,2,1024]{3,2,1,0:T(2,128)(2,1)}), bf16[16,32,2,1024]{3,2,1,0:T(2,128)(2,1)S(1)}, u32[]{:S(2)}, u32[]{:S(2)}) async-start(bf16[16,32,2,1024]{3,2,1,0:T(2,128)(2,1)} %param.4), calls=%async_computation | async-start | bytes 4194304 | tf_op jit(solution)/shard_map/all_to_all | solution.py:374
  13.8 3.6 %copy-start.3 = (bf16[2,2048,512]{2,1,0:T(8,128)(2,1)S(1)}, bf16[2,2048,512]{2,1,0:T(8,128)(2,1)}, u32[]{:S(2)}) copy-start(bf16[2,2048,512]{2,1,0:T(8,128)(2,1)} %param.5) | copy-start | bytes 12582916
  49.2 12.2 %copy-start.1 = (bf16[2048,1024]{1,0:T(8,128)(2,1)S(1)}, bf16[2048,1024]{1,0:T(8,128)(2,1)}, u32[]{:S(2)}) copy-start(bf16[2048,1024]{1,0:T(8,128)(2,1)} %pad_maximum_fusion.h_ref) | copy-start | bytes 12582916
  50.2 28.6 %collective-permute-start.1 = (bf16[512,1024]{1,0:T(8,128)(2,1)S(1)}, bf16[512,1024]{1,0:T(8,128)(2,1)S(1)}, u32[]{:S(2)}, u32[]{:S(2)}) collective-permute-start(bf16[512,1024]{1,0:T(8,128)(2,1)S(1)} %bitcast.20), channel_id=1, source_target_pairs={{1,0},{2,1},{3,2},{4,3},{5,4},{6,5},{7,6},{8,7},{9,8},{10,9},{11,1... | collective-permute-start | bytes 3145736 | tf_op jit(solution)/shard_map/ppermute | solution.py:23
  61.0 17.8 %copy-start = (bf16[2048,1024]{1,0:T(8,128)(2,1)S(1)}, bf16[2048,1024]{1,0:T(8,128)(2,1)}, u32[]{:S(2)}) copy-start(bf16[2048,1024]{1,0:T(8,128)(2,1)} %pad_maximum_fusion.1.h_ref) | copy-start | bytes 12582916
  61.0 31.3 %collective-permute-start = (bf16[512,1024]{1,0:T(8,128)(2,1)S(1)}, bf16[512,1024]{1,0:T(8,128)(2,1)S(1)}, u32[]{:S(2)}, u32[]{:S(2)}) collective-permute-start(bf16[512,1024]{1,0:T(8,128)(2,1)S(1)} %bitcast.23), channel_id=1, source_target_pairs={{1,0},{2,1},{3,2},{4,3},{5,4},{6,5},{7,6},{8,7},{9,8},{10,9},{11,1... | collective-permute-start | bytes 3145736 | tf_op jit(solution)/shard_map/ppermute | solution.py:23
  78.8 13.6 %copy-start.2 = (bf16[2048,1024]{1,0:T(8,128)(2,1)}, bf16[2048,1024]{1,0:T(8,128)(2,1)S(1)}, u32[]{:S(2)}) copy-start(bf16[2048,1024]{1,0:T(8,128)(2,1)S(1)} %get-tuple-element.27.power_ref) | copy-start | bytes 12582916
